TPU v7x, 256 devices: a whole 4x4x8 slice. The times are simulated.
256 devices in a mesh: ctx: 64 (over y_lo, x, z), head: 4 (over y_hi, core).
Axes of the slice: x: 4, y: 4 (y_hi: 2, y_lo: 2; y = y_hi * 2 + y_lo), z: 8, core: 2. Of those that a mesh axis runs over, the one named last changes fastest.
Arguments:
- queries: bfloat16 [12288, 768], P(('ctx', 'head')), may hold values from -2.5 to 2.5
- keys: bfloat16 [12288, 768], P(('ctx', 'head')), may hold values from -2.5 to 2.5
- values: bfloat16 [12288, 768], P(('ctx', 'head')), may hold values from -6 to 6
- attended: bfloat16 [12288, 768], P(('ctx', 'head')), may hold values from -6 to 6
- grad_out: bfloat16 [12288, 768], P(('ctx', 'head')), may hold values from -6 to 6
- logsumexp: float32 [12288, 12], P('ctx', 'head'), may hold values from 5 to 8
Outputs:
- grad_queries: bfloat16 [12288, 768], P(('ctx', 'head'))
- grad_keys: bfloat16 [12288, 768], P(('ctx', 'head'))
- grad_values: bfloat16 [12288, 768], P(('ctx', 'head'))
All inputs are finite; a program needn't handle non-finite values.
Results may differ from a plain program's by a relative error of at most 0.0051.
Values may be sent and summed in bfloat16 or wider, within the bound.
A program may use at most 128 MiB of HBM per device.

v0:
```python
import jax
import jax.numpy as jnp
from jax import lax
from jax.sharding import PartitionSpec as P


def block_rows(length):
    for candidate in (2048, 1024, 512):
        return candidate
    return length


def over_blocks(advance, totals, tensors):
    length = tensors[0].shape[0]
    block_size = block_rows(length)
    stacked = tuple(
        (
            matrix.reshape((length // block_size, block_size) + matrix.shape[1:])
            for matrix in tensors
        )
    )

    def single(current, blocks):
        return (advance(current, blocks), None)

    return lax.scan(single, totals, stacked)[0]


def attend(query_part, grad_part, norm_part, delta_part, key_part, value_part, scaling):
    scores = (
        jnp.einsum("ahd,bhd->hab", query_part, key_part, preferred_element_type=jnp.float32)
        * scaling
    )
    weights = jnp.exp(scores - jnp.transpose(norm_part)[:, :, None])
    weights_low = weights.astype(jnp.bfloat16)
    dweights = jnp.einsum("ahd,bhd->hab", grad_part, value_part, preferred_element_type=jnp.float32)
    dscores = (weights * (dweights - jnp.transpose(delta_part)[:, :, None])).astype(jnp.bfloat16)
    return (weights_low, dscores)


def query_term(dscores, key_part, scaling):
    return (
        jnp.einsum("hab,bhd->ahd", dscores, key_part, preferred_element_type=jnp.float32) * scaling
    )


def key_terms(weights_low, dscores, query_part, grad_part, scaling):
    grad_key = (
        jnp.einsum("hab,ahd->bhd", dscores, query_part, preferred_element_type=jnp.float32)
        * scaling
    )
    grad_value = jnp.einsum(
        "hab,ahd->bhd", weights_low, grad_part, preferred_element_type=jnp.float32
    )
    return (grad_key, grad_value)


def local(queries, keys, values, attended, grad_out, logsumexp):
    heads_local = logsumexp.shape[1]
    group_size = lax.axis_size("head")
    width_local = queries.shape[1] // group_size
    head_width = width_local // heads_local
    scaling = head_width ** (-0.5)
    moved = (
        lax.all_to_all(queries, "head", split_axis=1, concat_axis=0, tiled=True),
        lax.all_to_all(keys, "head", split_axis=1, concat_axis=0, tiled=True),
        lax.all_to_all(values, "head", split_axis=1, concat_axis=0, tiled=True),
        lax.all_to_all(grad_out, "head", split_axis=1, concat_axis=0, tiled=True),
        lax.all_to_all(attended, "head", split_axis=1, concat_axis=0, tiled=True),
    )
    length = moved[0].shape[0]

    def split(piece):
        return piece.reshape(piece.shape[0], heads_local, head_width)

    local_q, local_k, local_v, local_g, local_o = [split(matrix) for matrix in moved]
    deltas = jnp.sum(local_g.astype(jnp.float32) * local_o.astype(jnp.float32), axis=2)
    zeros = jnp.zeros((length, heads_local, head_width), jnp.float32)

    def keys_step(grad_query, blocks):
        key_part, value_part = blocks
        dscores = attend(local_q, local_g, logsumexp, deltas, key_part, value_part, scaling)[1]
        return grad_query + query_term(dscores, key_part, scaling)

    def queries_step(totals, blocks):
        query_part, grad_part, norm_part, delta_part = blocks
        weights_low, dscores = attend(
            query_part, grad_part, norm_part, delta_part, local_k, local_v, scaling
        )
        grad_key, grad_value = key_terms(weights_low, dscores, query_part, grad_part, scaling)
        return (totals[0] + grad_key, totals[1] + grad_value)

    all_norms, all_deltas = (
        lax.all_gather(logsumexp, "ctx", axis=0, tiled=True),
        lax.all_gather(deltas, "ctx", axis=0, tiled=True),
    )
    pieces = (
        lax.all_gather(moved[1], "ctx", axis=0, tiled=True),
        lax.all_gather(moved[2], "ctx", axis=0, tiled=True),
    )
    key_piece, value_piece = [split(piece) for piece in pieces]
    grad_query = over_blocks(keys_step, zeros, (key_piece, value_piece))
    pieces = (
        lax.all_gather(moved[0], "ctx", axis=0, tiled=True),
        lax.all_gather(moved[3], "ctx", axis=0, tiled=True),
    )
    query_piece, grad_piece = [split(piece) for piece in pieces]
    grad_key, grad_value = over_blocks(
        queries_step, (zeros, zeros), (query_piece, grad_piece, all_norms, all_deltas)
    )
    query_low = grad_query.reshape(length, width_local).astype(jnp.bfloat16)
    key_low = grad_key.reshape(length, width_local).astype(jnp.bfloat16)
    value_low = grad_value.reshape(length, width_local).astype(jnp.bfloat16)
    grad_queries, grad_keys, grad_values = (
        lax.all_to_all(query_low, "head", split_axis=0, concat_axis=1, tiled=True),
        lax.all_to_all(key_low, "head", split_axis=0, concat_axis=1, tiled=True),
        lax.all_to_all(value_low, "head", split_axis=0, concat_axis=1, tiled=True),
    )
    return (grad_queries, grad_keys, grad_values)


def solution(mesh):
    in_specs = (
        P(("ctx", "head"), None),
        P(("ctx", "head"), None),
        P(("ctx", "head"), None),
        P(("ctx", "head"), None),
        P(("ctx", "head"), None),
        P("ctx", "head"),
    )
    out_specs = (P(("ctx", "head"), None), P(("ctx", "head"), None), P(("ctx", "head"), None))
    return jax.shard_map(local, mesh=mesh, in_specs=in_specs, out_specs=out_specs, check_vma=False)
```

profile of v0, /device:TPU:1, one launch (start us, length us, event | category | flops | bytes accessed | tf_op | source)
XLA Modules:
  0.0 1368.2 jit_solution(7273158289976480809)
XLA Ops:
  7.2 1.0 all_to_all.106
  8.3 11.1 all_to_all.137
  19.5 1.0 all_to_all.113
  20.5 8.9 all_to_all.138
  29.4 1.0 all_to_all.102
  30.5 8.8 all_to_all.139
  39.4 1.0 all_to_all.109
  40.5 10.2 all_to_all.140
  50.7 1.1 all_to_all.116
  52.4 4.9 all-to-all-start.4
  57.3 135.5 %all-gather = f32[64,192,3]{1,2,0:T(4,128)S(1)} all-gather(f32[1,192,3]{1,2,0:T(4,128)} %bitcast.128), channel_id=1, replica_groups=mesh['ctx'=64,'head'=4] {'ctx'}, dimensions={0}, use_global_device_ids=true | all-gather | bytes 149760 | tf_op jit(solution)/shard_map/all_gather | solution.py:94
  192.9 1.0 reshape.70
  194.4 127.4 %all-gather.1 = f32[64,192,3]{1,2,0:T(4,128)S(1)} all-gather(f32[1,192,3]{1,2,0:T(4,128)S(1)} %copy.110), channel_id=1, replica_groups=mesh['ctx'=64,'head'=4] {'ctx'}, dimensions={0}, use_global_device_ids=true | all-gather | bytes 149760 | tf_op jit(solution)/shard_map/all_gather | solution.py:95
  322.6 23.3 %reshape.85 = bf16[6,2048,3,64]{3,2,1,0:T(4,128)(2,1)} reshape(bf16[12288,192]{1,0:T(8,128)(2,1)} %all-gather.11.cloned.1.call-done) | data formatting | bytes 9437184 | tf_op jit(solution)/shard_map/reshape;reshape | solution.py:18
  345.9 17.8 %copy.112 = bf16[6,2048,3,64]{1,3,2,0:T(8,128)(2,1)} copy(bf16[6,2048,3,64]{3,2,1,0:T(4,128)(2,1)} %reshape.85) | data formatting | bytes 9437184
  363.7 231.7 %all-gather.13.cloned.1.call-done = bf16[12288,192]{1,0:T(8,128)(2,1)} async-done(((bf16[192,192]{1,0:T(8,128)(2,1)}), bf16[12288,192]{1,0:T(8,128)(2,1)}) %all-gather.13.cloned.1.call-update) | async-done | bytes 4718608 | tf_op jit(solution)/shard_map/all_gather | solution.py:105
  595.4 23.3 %reshape.86 = bf16[6,2048,3,64]{3,2,1,0:T(4,128)(2,1)} reshape(bf16[12288,192]{1,0:T(8,128)(2,1)} %all-gather.13.cloned.1.call-done) | data formatting | bytes 9437184 | tf_op jit(solution)/shard_map/reshape;reshape | solution.py:18
  618.6 17.8 %copy.115 = bf16[6,2048,3,64]{1,3,2,0:T(8,128)(2,1)} copy(bf16[6,2048,3,64]{3,2,1,0:T(4,128)(2,1)} %reshape.86) | data formatting | bytes 9437184
  636.4 74.3 %while.25 = (s32[]{:T(128)}, f32[192,3,64]{0,2,1:T(8,128)S(1)}, f32[192,3,64]{0,2,1:T(8,128)S(1)}, bf16[6,2048,3,64]{1,3,2,0:T(8,128)(2,1)}, bf16[192,3,64]{0,2,...) while((s32[]{:T(128)}, f32[192,3,64]{0,2,1:T(8,128)S(1)}, ...), condition=%wide.region_4.5_spmd.clone, body=%wide.region_3.4_spmd.clone.sunk | while | flops 613601280 | bytes 18311292 | solution.py:26
  636.4 4.1 fusion.84
  640.6 4.6 fusion.85
  645.2 3.6 fusion.86
  648.8 4.1 fusion.84
  653.0 4.6 fusion.85
  657.6 3.6 fusion.86
  661.2 4.1 fusion.84
  665.4 4.6 fusion.85
  670.0 3.6 fusion.86
  673.6 4.1 fusion.84
  677.8 4.6 fusion.85
  682.3 3.6 fusion.86
  686.0 4.1 fusion.84
  690.1 4.6 fusion.85
  694.7 3.6 fusion.86
  698.4 4.1 fusion.84
  702.5 4.6 fusion.85
  707.1 3.6 fusion.86
  710.9 0.8 copy.131
  711.7 47.2 %all-to-all-start.6 = ((bf16[4,48,192]{2,1,0:T(8,128)(2,1)}), bf16[4,48,192]{2,1,0:T(8,128)(2,1)S(1)}, u32[]{:S(2)}, u32[]{:S(2)}) async-start(bf16[4,48,192]{2,1,0:T(8,128)(2,1)} %copy.131), calls=%async_computation.6 | async-start | bytes 196608 | tf_op jit(solution)/shard_map/all_to_all | solution.py:116
  759.6 0.8 copy.132
  760.4 143.0 %all-gather.7.cloned.1.call-done = bf16[12288,192]{1,0:T(8,128)(2,1)} async-done(((bf16[192,192]{1,0:T(8,128)(2,1)}), bf16[12288,192]{1,0:T(8,128)(2,1)}) %all-gather.7.cloned.1.call-update) | async-done | bytes 4718608 | tf_op jit(solution)/shard_map/all_gather | solution.py:98
  903.4 23.3 %reshape.82 = bf16[6,2048,3,64]{3,2,1,0:T(4,128)(2,1)} reshape(bf16[12288,192]{1,0:T(8,128)(2,1)} %all-gather.7.cloned.1.call-done) | data formatting | bytes 9437184 | tf_op jit(solution)/shard_map/reshape;reshape | solution.py:18
  926.7 17.8 %copy.100 = bf16[6,2048,3,64]{1,3,2,0:T(8,128)(2,1)} copy(bf16[6,2048,3,64]{3,2,1,0:T(4,128)(2,1)} %reshape.82) | data formatting | bytes 9437184
  944.5 266.3 %all-gather.9.cloned.1.call-done = bf16[12288,192]{1,0:T(8,128)(2,1)} async-done(((bf16[192,192]{1,0:T(8,128)(2,1)}), bf16[12288,192]{1,0:T(8,128)(2,1)}) %all-gather.9.cloned.1.call-update) | async-done | bytes 4718608 | tf_op jit(solution)/shard_map/all_gather | solution.py:99
  1210.8 23.3 %reshape.83 = bf16[6,2048,3,64]{3,2,1,0:T(4,128)(2,1)} reshape(bf16[12288,192]{1,0:T(8,128)(2,1)} %all-gather.9.cloned.1.call-done) | data formatting | bytes 9437184 | tf_op jit(solution)/shard_map/reshape;reshape | solution.py:18
  1234.1 17.8 %copy.102 = bf16[6,2048,3,64]{1,3,2,0:T(8,128)(2,1)} copy(bf16[6,2048,3,64]{3,2,1,0:T(4,128)(2,1)} %reshape.83) | data formatting | bytes 9437184
  1251.9 45.7 %all-to-all-start.7 = ((bf16[4,48,192]{2,1,0:T(8,128)(2,1)}), bf16[4,48,192]{2,1,0:T(8,128)(2,1)S(1)}, u32[]{:S(2)}, u32[]{:S(2)}) async-start(bf16[4,48,192]{2,1,0:T(8,128)(2,1)} %copy.132), calls=%async_computation.7 | async-start | bytes 196608 | tf_op jit(solution)/shard_map/all_to_all | solution.py:117
  1297.6 52.6 %while.24 = (s32[]{:T(128)}, f32[192,3,64]{0,2,1:T(8,128)S(1)}, bf16[6,2048,3,64]{1,3,2,0:T(8,128)(2,1)}, bf16[192,3,64]{0,2,1:T(8,128)(2,1)S(1)}, f32[192,3]{0,...) while((s32[]{:T(128)}, f32[192,3,64]{0,2,1:T(8,128)S(1)}, ...), condition=%wide.region_2.3_spmd.clone, body=%wide.region_1.2_spmd.clone.sunk | while | flops 458993664 | bytes 12245103 | solution.py:26
  1297.6 4.1 fusion.75
  1301.7 4.7 fusion.76
  1306.4 4.1 fusion.75
  1310.5 4.7 fusion.76
  1315.1 4.1 fusion.75
  1319.2 4.7 fusion.76
  1323.9 4.1 fusion.75
  1328.0 4.7 fusion.76
  1332.7 4.1 fusion.75
  1336.8 4.7 fusion.76
  1341.4 4.1 fusion.75
  1345.5 4.7 fusion.76
  1350.4 0.8 copy.126
  1351.2 4.8 all-to-all-start.5
  1356.8 0.7 all_to_all.128
  1357.6 3.2 all-to-all-done.5
  (73 shorter events, 5.4 us)
Async XLA Ops:
  7.2 315.4 %all-gather.11.cloned.1.call-start = ((), (), s32[]{:S(2)}) async-start(), calls=%async_computation.10 | async-start | bytes 6389760 | tf_op jit(solution)/shard_map/all_gather | solution.py:104
  19.4 575.9 %all-gather.13.cloned.1.call-start = ((), (), s32[]{:S(2)}) async-start(), calls=%async_computation.11 | async-start | bytes 6389760 | tf_op jit(solution)/shard_map/all_gather | solution.py:105
  29.4 874.0 %all-gather.7.cloned.1.call-start = ((), (), s32[]{:S(2)}) async-start(), calls=%async_computation.8 | async-start | bytes 6389760 | tf_op jit(solution)/shard_map/all_gather | solution.py:98
  39.3 282.7 %copy-start.1 = (bf16[48,4,192]{2,0,1:T(8,128)(2,1)S(1)}, bf16[48,4,192]{2,0,1:T(8,128)(2,1)}, u32[]{:S(2)}) copy-start(bf16[48,4,192]{2,0,1:T(8,128)(2,1)} %all_to_all.139) | copy-start | bytes 221188
  39.4 1171.4 %all-gather.9.cloned.1.call-start = ((), (), s32[]{:S(2)}) async-start(), calls=%async_computation.9 | async-start | bytes 6389760 | tf_op jit(solution)/shard_map/all_gather | solution.py:99
  50.6 271.7 %copy-start.2 = (bf16[48,4,192]{2,0,1:T(8,128)(2,1)S(1)}, bf16[48,4,192]{2,0,1:T(8,128)(2,1)}, u32[]{:S(2)}) copy-start(bf16[48,4,192]{2,0,1:T(8,128)(2,1)} %all_to_all.140) | copy-start | bytes 221188
  52.4 141.5 %all-to-all-start.4 = ((bf16[48,4,192]{2,0,1:T(8,128)(2,1)}), bf16[48,4,192]{2,0,1:T(8,128)(2,1)S(1)}, u32[]{:S(2)}, u32[]{:S(2)}) async-start(bf16[48,4,192]{2,0,1:T(8,128)(2,1)} %copy.99), calls=%async_computation.4 | async-start | bytes 196608 | tf_op jit(solution)/shard_map/all_to_all | solution.py:69
  636.4 122.7 %copy-start = (bf16[48,4,192]{2,0,1:T(8,128)(2,1)S(1)}, bf16[48,4,192]{2,0,1:T(8,128)(2,1)}, u32[]{:S(2)}) copy-start(bf16[48,4,192]{2,0,1:T(8,128)(2,1)} %all_to_all.137) | copy-start | bytes 221188
  711.7 540.2 %all-to-all-start.6 = ((bf16[4,48,192]{2,1,0:T(8,128)(2,1)}), bf16[4,48,192]{2,1,0:T(8,128)(2,1)S(1)}, u32[]{:S(2)}, u32[]{:S(2)}) async-start(bf16[4,48,192]{2,1,0:T(8,128)(2,1)} %copy.131), calls=%async_computation.6 | async-start | bytes 196608 | tf_op jit(solution)/shard_map/all_to_all | solution.py:116
  1234.1 63.5 %copy-start.3 = (f32[192,3]{0,1:T(4,128)S(1)}, f32[192,3]{0,1:T(4,128)}, u32[]{:S(2)}) copy-start(f32[192,3]{0,1:T(4,128)} %param.15) | copy-start | bytes 6916
  1251.9 99.3 %all-to-all-start.7 = ((bf16[4,48,192]{2,1,0:T(8,128)(2,1)}), bf16[4,48,192]{2,1,0:T(8,128)(2,1)S(1)}, u32[]{:S(2)}, u32[]{:S(2)}) async-start(bf16[4,48,192]{2,1,0:T(8,128)(2,1)} %copy.132), calls=%async_computation.7 | async-start | bytes 196608 | tf_op jit(solution)/shard_map/all_to_all | solution.py:117
  1351.2 9.7 all-to-all-start.5
Sparse Core Ops, SparseCore 0:
  19.5 266.6 all-gather.10
  288.0 307.3 all-gather.12
  597.1 306.2 all-gather.6
  905.0 305.7 all-gather.8
where the time goes:
time: 1370 us
  waiting for transfers between devices  644 us (47%)
  blocking collectives  302 us (22%)
  local copies, waits for them, and re-layouts  178 us (13%)
  matrix products  126 us (9%)
  starting transfers between devices  103 us (8%)
  between operations  14 us (1%)
    all_gather x1, waiting for transfers between devices, local(): lax.all_gather(moved[2], 'ctx', axis=0, tiled=True)  266 us
    all_gather x1, waiting for transfers between devices, local(): lax.all_gather(moved[3], 'ctx', axis=0, tiled=True)  232 us
    all_gather x1, waiting for transfers between devices, local(): lax.all_gather(moved[1], 'ctx', axis=0, tiled=True)  143 us
    all_gather x1, blocking collectives, local(): lax.all_gather(logsumexp, 'ctx', axis=0, tiled=True)  135 us
    all_gather x1, blocking collectives, local(): lax.all_gather(deltas, 'ctx', axis=0, tiled=True)  127 us
    another operation x4, local copies, waits for them, and re-layouts, over_blocks(): matrix.reshape((length // block_size, block_size) + matrix.shape[1:])  93 us
    unnamed x18, local copies, waits for them, and re-layouts  72.1 us
    dot_general x12, matrix products, attend(): jnp.einsum('ahd,bhd->hab', query_part, key_part, preferred_element_type=j...  49 us
  transfers between devices with their start and end apart: 8, of which 4 were waited for; matrix products, arithmetic and copies ran while one was open for 22% of the time, Pallas kernels for 0%

commit v1 on v0

v1 whole, which is shorter than its diff:
```python
import functools

import jax
import jax.numpy as jnp
from jax import lax
from jax.experimental import pallas as pl
from jax.experimental.pallas import tpu as pltpu
from jax.sharding import PartitionSpec as P

F32 = jnp.float32
BF16 = jnp.bfloat16
MESH = pl.DeviceIdType.MESH

NX, NY, NZ = 4, 4, 8
HL = 3
D = 64
SUB = 48
CH = NY * SUB
NI = NZ * CH
NJ = 2 * NX * CH
HALF = NJ // 2
Z_SLOT = {0: 0, 1: 1, -1: 2, 2: 3, -2: 4, 3: 5, -3: 6, 4: 7}
X_SLOT = {0: 0, 1: 1, -1: 2, 2: 3}
PK = CH + CH // 2
BJ = 512


def nt(a, b):
    return lax.dot_general(a, b, (((1,), (1,)), ((), ())), preferred_element_type=F32)


def tn(a, b):
    return lax.dot_general(a, b, (((0,), (0,)), ((), ())), preferred_element_type=F32)


def nn(a, b):
    return jnp.dot(a, b, preferred_element_type=F32)


def kernel(
    q_ref, k_ref, v_ref, o_ref, g_ref, lse_ref, dq_ref, dk_ref, dv_ref,
    st_qg, st_kv, st_d, qg, kv, r_lse, r_d, stat, stat_all, dqt, dkv, dkv16, r_core, x16, r_x,
    dq16, r_q, fin, r_fin,
    a_send, a_recv, l_send, l_recv, z_send, z_recv, x_send, x_recv, c_send, c_recv,
    kc_send, kc_recv, kx_send, kx_recv, q_send, q_recv, f_send, f_recv,
):
    c = lax.axis_index("ctx")
    g = lax.axis_index("head")
    z = c % NZ
    x = (c // NZ) % NX
    y_lo = c // (NZ * NX)
    y_hi = g // 2
    core = g % 2
    y = 2 * y_hi + y_lo

    def dev(dx=0, dy=0, dz=0, other=False):
        yy = (y + dy) % NY
        cc = (yy % 2) * (NX * NZ) + ((x + dx + NX) % NX) * NZ + (z + dz + NZ) % NZ
        return (cc, (yy // 2) * 2 + (1 - core if other else core))

    def remote(src, dst, send, recv, to):
        return pltpu.make_async_remote_copy(
            src_ref=src, dst_ref=dst, send_sem=send, recv_sem=recv, device_id=to,
            device_id_type=MESH,
        )

    barrier = pltpu.get_barrier_semaphore()
    peers = [dev(dy=dy, other=o) for dy in range(NY) for o in (False, True) if dy or o]
    peers += [dev(dz=d) for d in Z_SLOT if d] + [dev(dx=d) for d in X_SLOT if d]
    for peer in peers:
        pl.semaphore_signal(barrier, inc=1, device_id=peer, device_id_type=MESH)

    qs = q_ref[...] * jnp.asarray(0.125, BF16)
    ks, vs, gs = k_ref[...], v_ref[...], g_ref[...]
    for n in range(NY * HL):
        cols = slice(n * D, (n + 1) * D)
        st_qg[n // HL, n % HL] = jnp.concatenate([qs[:, cols], gs[:, cols]], axis=1)
        st_kv[n // HL, n % HL] = jnp.concatenate([ks[:, cols], vs[:, cols]], axis=1)
    prod = gs.astype(F32) * o_ref[...].astype(F32)
    hi = prod.astype(BF16)
    lo = (prod - hi.astype(F32)).astype(BF16)
    row = lax.broadcasted_iota(jnp.int32, (8 * NY, NY * HL * D), 0)
    col = lax.broadcasted_iota(jnp.int32, (8 * NY, NY * HL * D), 1)
    start = ((row // 8) * HL + row % 8) * D
    pick = ((row % 8 < HL) & (col >= start) & (col < start + D)).astype(F32).astype(BF16)
    deltas = nt(pick, hi) + nt(pick, lo)
    for n in range(NY):
        st_d[n] = deltas[8 * n : 8 * n + 8]

    pl.semaphore_wait(barrier, len(peers))

    first = []
    for r in range(1, NY):
        to = dev(dy=r)
        group = (y + r) % NY
        rows = pl.ds((NY - r) * SUB, SUB)
        first += [
            remote(st_qg.at[group], qg.at[:, rows], a_send.at[r, 0], a_recv.at[r, 0], to),
            remote(st_kv.at[group], kv.at[:, rows], a_send.at[r, 1], a_recv.at[r, 1], to),
            remote(st_d.at[group], r_d.at[NY - r], a_send.at[r, 2], a_recv.at[r, 2], to),
        ]
    for copy in first:
        copy.start()
    lse_to = (g % 2) * (NX * NZ) + x * NZ + z
    lse_own = core == y_lo

    def lse_copy(score):
        return remote(
            lse_ref.at[score], r_lse.at[y_lo], l_send.at[score], l_recv.at[y_lo],
            (lse_to, (g // 2) * 2 + score),
        )

    def lse_local(score):
        return lse_own & (core == score)

    for score in range(2):

        @pl.when(jnp.logical_not(lse_local(score)))
        def _():
            lse_copy(score).start()

        @pl.when(lse_local(score))
        def _():
            r_lse[y_lo] = lse_ref[score]

    qg[:, 0:SUB] = st_qg[y]
    kv[:, 0:SUB] = st_kv[y]
    r_d[0] = st_d[y]
    for copy in first:
        copy.wait_recv()
    for source in range(2):

        @pl.when(jnp.logical_not(lse_own & (source == y_lo)))
        def _():
            remote(
                lse_ref.at[0], r_lse.at[source], l_send.at[0], l_recv.at[source],
                (lse_to, (g // 2) * 2),
            ).wait_recv()

    for r in range(NY):
        from_y = (y + r) % NY
        stat[0, 0:8, r * SUB : (r + 1) * SUB] = r_lse[from_y % 2, from_y // 2]
        stat[0, 8:16, r * SUB : (r + 1) * SUB] = r_d[r]

    def z_copies(step, sign):
        d = -sign * (step - 1)
        arrives = d - sign
        if step == NZ // 2:
            arrives, part = 4, CH // 2
            offset = 0 if sign > 0 else part
        else:
            part, offset = CH, 0
        a, b = Z_SLOT[d], Z_SLOT[arrives]
        way = 0 if sign > 0 else 1
        copies = [
            remote(
                qg.at[:, pl.ds(a * CH + offset, part)], qg.at[:, pl.ds(b * CH + offset, part)],
                z_send.at[way, step, 0], z_recv.at[way, step, 0], dev(dz=sign),
            )
        ]
        if step < NZ // 2 or sign > 0:
            copies.append(
                remote(
                    stat.at[a], stat.at[b], z_send.at[way, step, 1], z_recv.at[way, step, 1],
                    dev(dz=sign),
                )
            )
        return copies

    def x_copies(step, sign):
        d = -sign * (step - 1)
        arrives = d - sign
        if step == NX // 2:
            arrives, part = 2, CH // 2
            offset = 0 if sign > 0 else part
        else:
            part, offset = CH, 0
        a, b = X_SLOT[d], X_SLOT[arrives]
        way = 0 if sign > 0 else 1
        return [
            remote(
                kv.at[:, pl.ds(a * CH + offset, part)], kv.at[:, pl.ds(b * CH + offset, part)],
                x_send.at[way, step], x_recv.at[way, step], dev(dx=sign),
            )
        ]

    def core_copy(slot):
        return remote(
            kv.at[:, pl.ds(slot * CH, CH)], kv.at[:, pl.ds(HALF + slot * CH, CH)],
            c_send.at[slot], c_recv.at[slot], dev(other=True),
        )

    sent = []
    zs = {}
    for step in range(1, NZ // 2 + 1):
        for sign in (1, -1):
            if step > 1:
                for copy in zs[step - 1, sign]:
                    copy.wait_recv()
            zs[step, sign] = z_copies(step, sign)
            for copy in zs[step, sign]:
                copy.start()
            sent += zs[step, sign]
        if step == 1:
            xs = x_copies(1, 1) + x_copies(1, -1) + [core_copy(0)]
            for copy in xs:
                copy.start()
        if step == 2:
            xs[0].wait_recv()
            xs[1].wait_recv()
            more = x_copies(2, 1) + x_copies(2, -1) + [core_copy(1), core_copy(2)]
            for copy in more:
                copy.start()
        if step == 3:
            more[0].wait_recv()
            more[1].wait_recv()
            last = core_copy(3)
            last.start()
    for sign in (1, -1):
        for copy in zs[NZ // 2, sign]:
            copy.wait_recv()
    for copy in [xs[2], more[2], more[3], last]:
        copy.wait_recv()
    sent += xs + more + [last]
    for slot in range(NZ):
        stat_all[:, slot * CH : (slot + 1) * CH] = stat[slot]

    lane = lax.broadcasted_iota(jnp.int32, (BJ, 2 * D), 1)

    @pl.loop(0, HL)
    def _(h):
        norms = stat_all[pl.ds(h, 1), :]
        dels = stat_all[pl.ds(8 + h, 1), :]
        rows_q = qg[h]
        for jb in range(NJ // BJ):
            js = slice(jb * BJ, (jb + 1) * BJ)
            both = kv[h, js]
            zero = jnp.zeros_like(both)
            scores = nt(jnp.where(lane < D, both, zero), rows_q)
            dweights = nt(jnp.where(lane < D, zero, both), rows_q)
            weights = jnp.exp(scores - norms)
            dscores = (weights * (dweights - dels)).astype(BF16)
            low = weights.astype(BF16)
            dkv[h, js] = jnp.where(lane < D, nn(dscores, rows_q), nn(low, rows_q))
            term = tn(both, dscores)[:D]
            if jb == 0:
                dqt[h] = term
            else:
                dqt[h] += term

    dkv16[...] = dkv[:, HALF:].astype(BF16)
    kc = remote(dkv16, r_core, kc_send, kc_recv, dev(other=True))
    kc.start()
    for s in range(NI // 384):
        block = jnp.transpose(dqt[:, :, s * 384 : (s + 1) * 384].reshape(HL * D, 384))
        block = (block * 0.125).astype(BF16)
        for t in range(2):
            piece = block[t * CH : (t + 1) * CH]
            dq16[2 * s + t, 0:CH] = piece[:, : 2 * D]
            dq16[2 * s + t, CH:PK] = jnp.concatenate(
                [piece[: CH // 2, 2 * D :], piece[CH // 2 :, 2 * D :]], axis=1
            )
    qc = []
    for d, slot in Z_SLOT.items():
        if d:
            back = Z_SLOT[4 if d == 4 else -d]
            qc.append(
                remote(dq16.at[slot], r_q.at[back], q_send.at[slot], q_recv.at[slot], dev(dz=d))
            )
    for copy in qc:
        copy.start()
    kc.wait_recv()
    dkv[:, :HALF] = dkv[:, :HALF] + r_core[...].astype(F32)
    x16[...] = dkv[:, CH:HALF].astype(BF16)
    xc = []
    for d, slot in X_SLOT.items():
        if d:
            back = X_SLOT[2 if d == 2 else -d]
            xc.append(
                remote(
                    x16.at[:, pl.ds((slot - 1) * CH, CH)], r_x.at[back - 1], kx_send.at[slot],
                    kx_recv.at[slot], dev(dx=d),
                )
            )
    for copy in xc:
        copy.start()
    for copy in qc:
        copy.wait_recv()
    total_q = dq16[0].astype(F32)
    for slot in range(1, NZ):
        total_q = total_q + r_q[slot].astype(F32)
    for copy in xc:
        copy.wait_recv()
    for r in range(NY):
        rows = slice(r * SUB, (r + 1) * SUB)
        for h in range(HL):
            total = dkv[h, rows]
            for slot in range(NX - 1):
                total = total + r_x[slot, h, rows].astype(F32)
            fin[r, :, h * 2 * D : (h + 1) * 2 * D] = total.astype(BF16)
        fin[r, :, 6 * D : 8 * D] = total_q[rows].astype(BF16)
        at = CH + (r % 2) * SUB
        side = total_q[at : at + SUB]
        fin[r, :, 8 * D : 9 * D] = side[:, (r // 2) * D : (r // 2 + 1) * D].astype(BF16)

    fc = [
        remote(fin.at[r], r_fin.at[y], f_send.at[r], f_recv.at[r], dev(dy=r)) for r in range(1, NY)
    ]
    for copy in fc:
        copy.start()
    r_fin[y] = fin[0]
    for copy in fc:
        copy.wait_recv()
    for n in range(NY):
        for h in range(HL):
            cols = slice((n * HL + h) * D, (n * HL + h + 1) * D)
            pair = r_fin[n, :, h * 2 * D : (h + 1) * 2 * D]
            dk_ref[:, cols] = pair[:, :D]
            dv_ref[:, cols] = pair[:, D:]
            dq_ref[:, cols] = r_fin[n, :, (6 + h) * D : (7 + h) * D]
    for copy in first + sent + [kc] + qc + xc + fc:
        copy.wait_send()
    for score in range(2):

        @pl.when(jnp.logical_not(lse_local(score)))
        def _():
            lse_copy(score).wait_send()


def local(queries, keys, values, attended, grad_out, logsumexp):
    norms = jnp.pad(jnp.transpose(logsumexp), ((0, 8 - HL), (0, 0)))
    norms = norms.reshape(8, 2, 2, SUB).transpose(2, 1, 0, 3)
    out = jax.ShapeDtypeStruct(queries.shape, BF16)
    dma = pltpu.SemaphoreType.DMA
    vm = pltpu.VMEM
    return pl.pallas_call(
        kernel,
        out_shape=(out, out, out),
        in_specs=[pl.BlockSpec(memory_space=pltpu.VMEM)] * 6,
        out_specs=[pl.BlockSpec(memory_space=pltpu.VMEM)] * 3,
        scratch_shapes=[
            vm((NY, HL, SUB, 2 * D), BF16),
            vm((NY, HL, SUB, 2 * D), BF16),
            vm((NY, 8, SUB), F32),
            vm((HL, NI, 2 * D), BF16),
            vm((HL, NJ, 2 * D), BF16),
            vm((2, 2, 8, SUB), F32),
            vm((NY, 8, SUB), F32),
            vm((NZ, 16, CH), F32),
            vm((16, NI), F32),
            vm((HL, D, NI), F32),
            vm((HL, NJ, 2 * D), F32),
            vm((HL, HALF, 2 * D), BF16),
            vm((HL, HALF, 2 * D), BF16),
            vm((HL, HALF - CH, 2 * D), BF16),
            vm((NX - 1, HL, CH, 2 * D), BF16),
            vm((NZ, PK, 2 * D), BF16),
            vm((NZ, PK, 2 * D), BF16),
            vm((NY, SUB, 10 * D), BF16),
            vm((NY, SUB, 10 * D), BF16),
            dma((NY, 3)), dma((NY, 3)),
            dma((2,)), dma((2,)),
            dma((2, NZ // 2 + 1, 2)), dma((2, NZ // 2 + 1, 2)),
            dma((2, NX // 2 + 1)), dma((2, NX // 2 + 1)),
            dma((NX,)), dma((NX,)),
            dma, dma,
            dma((NX,)), dma((NX,)),
            dma((NZ,)), dma((NZ,)),
            dma((NY,)), dma((NY,)),
        ],
        compiler_params=pltpu.CompilerParams(
            collective_id=0, has_side_effects=True, vmem_limit_bytes=56 << 20
        ),
        name="attention_grad",
    )(queries, keys, values, attended, grad_out, norms)


def solution(mesh):
    rows = P(("ctx", "head"), None)
    return jax.shard_map(
        local,
        mesh=mesh,
        in_specs=(rows,) * 5 + (P("ctx", "head"),),
        out_specs=(rows,) * 3,
        check_vma=False,
    )
```

time: 1370 us -> 77.1 us (0.06)
  the two profiles are of different devices: /device:TPU:1 before, /device:TPU:2 now
where the time goes in v1:
time: 77.1 us; the launch traced here: 76.8 us
  Pallas kernels  71.7 us (93%)
  local copies, waits for them, and re-layouts  4.49 us (6%)
    pallas_call x1, Pallas kernels, local(): pl.pallas_call(kernel, out_shape=(out, out, out), in_specs=[pl.BlockSpec(...  71.7 us
    unnamed x7, local copies, waits for them, and re-layouts  3.1 us

profile of v1, /device:TPU:2, one launch (start us, length us, event | category | flops | bytes accessed | tf_op | source)
XLA Modules:
  0.0 76.8 jit_solution(9587296770336186757)
XLA Ops:
  0.6 0.7 pad.4
  1.3 0.1 reshape.9
  1.4 0.6 copy.11
  2.0 71.7 %attention_grad.1 = (bf16[48,768]{1,0:T(8,128)(2,1)}, bf16[48,768]{1,0:T(8,128)(2,1)}, bf16[48,768]{1,0:T(8,128)(2,1)}) custom-call(bf16[48,768]{1,0:T(8,128)(2,1)} %q_ref.1, bf16[48,768]{1,0:T(8,128)(2,1)} %k_ref.1, bf16[48,768]{1,0:T(8,128)(2,1)} %v_ref.1, bf16[48,768]{1,0:T(8,128)(2,1)} %o_ref.1, bf16[48,768]{1,0:T(8,128)(2,1)} %g_ref.1, ...), custom_call_target="tpu_custom_call" | custom-call | tf_op jit(solution)/shard_map/attention_grad/pallas_call | solution.py:336
  73.7 0.0 copy-start.1
  73.7 1.6 %copy.15 = bf16[48,768]{1,0:T(8,128)(2,1)} copy(bf16[48,768]{1,0:T(8,128)(2,1)} %get-tuple-element.6) | data formatting | bytes 147456
  75.3 0.0 copy-done.1
  75.3 0.0 copy-start
  75.3 0.6 copy.16
  75.9 0.3 copy-done
  76.2 0.6 copy.17
Async XLA Ops:
  73.7 1.6 %copy-start.1 = (bf16[48,768]{1,0:T(8,128)(2,1)S(1)}, bf16[48,768]{1,0:T(8,128)(2,1)}, u32[]{:S(2)}) copy-start(bf16[48,768]{1,0:T(8,128)(2,1)} %get-tuple-element.7) | copy-start | bytes 221188
  75.3 0.9 %copy-start = (bf16[48,768]{1,0:T(8,128)(2,1)S(1)}, bf16[48,768]{1,0:T(8,128)(2,1)}, u32[]{:S(2)}) copy-start(bf16[48,768]{1,0:T(8,128)(2,1)} %get-tuple-element.8) | copy-start | bytes 221188

commit v2 on v0

v2 whole, which is shorter than its diff:
```python
import functools

import jax
import jax.numpy as jnp
from jax import lax
from jax.experimental import pallas as pl
from jax.experimental.pallas import tpu as pltpu
from jax.sharding import PartitionSpec as P

F32 = jnp.float32
BF16 = jnp.bfloat16
MESH = pl.DeviceIdType.MESH

NX, NY, NZ = 4, 4, 8
HL = 3
D = 64
SUB = 48
CH = NY * SUB
NI = NZ * CH
NJ = 2 * NX * CH
HALF = NJ // 2
Z_SLOT = {0: 0, 1: 1, -1: 2, 2: 3, -2: 4, 3: 5, -3: 6, 4: 7}
X_SLOT = {0: 0, 1: 1, -1: 2, 2: 3}
PK = CH // 2


def nt(a, b):
    return lax.dot_general(a, b, (((1,), (1,)), ((), ())), preferred_element_type=F32)


def tn(a, b):
    return lax.dot_general(a, b, (((0,), (0,)), ((), ())), preferred_element_type=F32)


def nn(a, b):
    return jnp.dot(a, b, preferred_element_type=F32)


def kernel(
    q_ref, k_ref, v_ref, o_ref, g_ref, lse_ref, out_kv, out_q,
    st_qg, st_kv, st_d, st_lse, qg, kv, r_lse, r_d, stat, stat_all, dqt, dkv, dkv16, r_core, x16,
    r_x, dq16, r_q, fin_kv, fin_q, r_kv, r_fq,
    a_send, a_recv, l_send, l_recv, z_send, z_recv, s_send, s_recv, x_send, x_recv, c_send, c_recv,
    kc_send, kc_recv, kx_send, kx_recv, q_send, q_recv, f_send, f_recv,
):
    c = lax.axis_index("ctx")
    g = lax.axis_index("head")
    z = c % NZ
    x = (c // NZ) % NX
    y_lo = c // (NZ * NX)
    y_hi = g // 2
    core = g % 2
    y = 2 * y_hi + y_lo

    def dev(dx=0, dy=0, dz=0, other=False):
        yy = (y + dy) % NY
        cc = (yy % 2) * (NX * NZ) + ((x + dx + NX) % NX) * NZ + (z + dz + NZ) % NZ
        return (cc, (yy // 2) * 2 + (1 - core if other else core))

    def remote(src, dst, send, recv, to):
        return pltpu.make_async_remote_copy(
            src_ref=src, dst_ref=dst, send_sem=send, recv_sem=recv, device_id=to,
            device_id_type=MESH,
        )

    def start(copies):
        for copy in copies:
            copy.start()

    def arrive(copies):
        for copy in copies:
            copy.wait_recv()

    barrier = pltpu.get_barrier_semaphore()
    peers = [dev(dy=dy, other=o) for dy in range(NY) for o in (False, True) if dy or o]
    peers += [dev(dz=d) for d in Z_SLOT if d] + [dev(dx=d) for d in X_SLOT if d]
    for peer in peers:
        pl.semaphore_signal(barrier, inc=1, device_id=peer, device_id_type=MESH)

    def y_copy(r, kind):
        group = (y + r) % NY
        rows = pl.ds((NY - r) * SUB, SUB)
        src = (st_qg, st_kv, st_d)[kind].at[group]
        dst = (qg.at[:, rows], kv.at[:, rows], r_d.at[NY - r])[kind]
        return remote(src, dst, a_send.at[r, kind], a_recv.at[r, kind], dev(dy=r))

    def ring(buf, slots, axis, last, step, sign, r, send, recv):
        d = -sign * (step - 1)
        a = slots[d]
        b = slots[last if step == last else d - sign]
        way = 0 if sign > 0 else 1
        return remote(
            buf.at[:, pl.ds(a * CH + r * SUB, SUB)], buf.at[:, pl.ds(b * CH + r * SUB, SUB)],
            send.at[way, step, r], recv.at[way, step, r], dev(**{axis: sign}),
        )

    def z_copy(step, sign, r):
        return ring(qg, Z_SLOT, "dz", NZ // 2, step, sign, r, z_send, z_recv)

    def x_copy(step, sign, r):
        return ring(kv, X_SLOT, "dx", NX // 2, step, sign, r, x_send, x_recv)

    def halves(step, last, sign):
        return range(NY) if step < last else ((0, 1) if sign > 0 else (2, 3))

    def s_copy(step, sign):
        d = -sign * (step - 1)
        way = 0 if sign > 0 else 1
        return remote(
            stat.at[Z_SLOT[d]], stat.at[Z_SLOT[4 if step == NZ // 2 else d - sign]],
            s_send.at[way, step], s_recv.at[way, step], dev(dz=sign),
        )

    def c_copy(i):
        begin, rows = [(r * SUB, SUB) for r in range(NY)][i] if i < NY else (
            ((i - 3) * CH, CH) if i < 6 else (3 * CH + (i - 6) * (CH // 2), CH // 2)
        )
        return remote(
            kv.at[:, pl.ds(begin, rows)], kv.at[:, pl.ds(HALF + begin, rows)],
            c_send.at[i], c_recv.at[i], dev(other=True),
        )

    lse_to = (g % 2) * (NX * NZ) + x * NZ + z
    lse_own = core == y_lo

    def lse_copy(score):
        return remote(
            st_lse.at[score], r_lse.at[y_lo], l_send.at[score], l_recv.at[y_lo],
            (lse_to, (g // 2) * 2 + score),
        )

    def lse_local(score):
        return lse_own & (core == score)

    def stage(st, left, right):
        for n in range(NY * HL):
            cols = slice(n * D, (n + 1) * D)
            st[n // HL, n % HL] = jnp.concatenate([left[:, cols], right[:, cols]], axis=1)

    order = (1, 3, 2)
    stage(st_kv, k_ref[...], v_ref[...])
    pl.semaphore_wait(barrier, len(peers))
    start([y_copy(r, 1) for r in order])
    kv[:, 0:SUB] = st_kv[y]
    start([x_copy(1, 1, 0), x_copy(1, -1, 0), c_copy(0)])
    gs = g_ref[...]
    stage(st_qg, q_ref[...] * jnp.asarray(0.125, BF16), gs)
    start([y_copy(r, 0) for r in order])
    qg[:, 0:SUB] = st_qg[y]
    start([z_copy(1, 1, 0), z_copy(1, -1, 0)])
    prod = gs.astype(F32) * o_ref[...].astype(F32)
    hi = prod.astype(BF16)
    lo = (prod - hi.astype(F32)).astype(BF16)
    row = lax.broadcasted_iota(jnp.int32, (8 * NY, NY * HL * D), 0)
    col = lax.broadcasted_iota(jnp.int32, (8 * NY, NY * HL * D), 1)
    begin = ((row // 8) * HL + row % 8) * D
    pick = ((row % 8 < HL) & (col >= begin) & (col < begin + D)).astype(F32).astype(BF16)
    deltas = nt(pick, hi) + nt(pick, lo)
    for n in range(NY):
        st_d[n] = deltas[8 * n : 8 * n + 8]
    start([y_copy(r, 2) for r in order])
    st_lse[...] = jnp.zeros_like(st_lse)
    for s in range(NY):
        st_lse[s % 2, s // 2, 0:HL] = lse_ref[:, s * SUB : (s + 1) * SUB]
    for score in range(2):

        @pl.when(jnp.logical_not(lse_local(score)))
        def _():
            lse_copy(score).start()

        @pl.when(lse_local(score))
        def _():
            r_lse[y_lo] = st_lse[score]

    r_d[0] = st_d[y]
    dqt[...] = jnp.zeros_like(dqt)
    dkv[...] = jnp.zeros_like(dkv)

    for r, kind in ((1, 1), (3, 1), (1, 0), (3, 0), (2, 1), (2, 0)):
        y_copy(NY - r, kind).wait_recv()
        if kind == 1:
            start([x_copy(1, 1, r), x_copy(1, -1, r), c_copy(r)])
        else:
            start([z_copy(1, 1, r), z_copy(1, -1, r)])
    for r in range(1, NY):
        y_copy(r, 2).wait_recv()
    for source in range(2):

        @pl.when(jnp.logical_not(lse_own & (source == y_lo)))
        def _():
            remote(
                st_lse.at[0], r_lse.at[source], l_send.at[0], l_recv.at[source],
                (lse_to, (g // 2) * 2),
            ).wait_recv()

    for r in range(NY):
        from_at = (y + r) % NY
        stat[0, 0:8, r * SUB : (r + 1) * SUB] = r_lse[from_at % 2, from_at // 2]
        stat[0, 8:16, r * SUB : (r + 1) * SUB] = r_d[r]
    start([s_copy(1, 1), s_copy(1, -1)])
    for r in (0, 1, 3, 2):
        for sign in (1, -1):
            x_copy(1, sign, r).wait_recv()
            if r in halves(2, 2, sign):
                x_copy(2, sign, r).start()
        for sign in (1, -1):
            z_copy(1, sign, r).wait_recv()
            z_copy(2, sign, r).start()
    start([c_copy(4), c_copy(5)])
    for sign in (1, -1):
        s_copy(1, sign).wait_recv()
        s_copy(2, sign).start()
    for sign, i in ((1, 6), (-1, 7)):
        arrive([x_copy(2, sign, r) for r in halves(2, 2, sign)])
        c_copy(i).start()
    for r in (0, 1, 3, 2):
        for sign in (1, -1):
            z_copy(2, sign, r).wait_recv()
            z_copy(3, sign, r).start()
    for sign in (1, -1):
        s_copy(2, sign).wait_recv()
        s_copy(3, sign).start()

    def join(slots):
        for slot in slots:
            stat_all[:, slot * CH : (slot + 1) * CH] = stat[slot]

    join(range(4))

    def q_copy(h, d):
        slot = Z_SLOT[d]
        back = Z_SLOT[4 if d == 4 else -d]
        return remote(
            dq16.at[h, slot], r_q.at[h, back], q_send.at[h, slot], q_recv.at[h, slot], dev(dz=d)
        )

    def send_dq(h, half):
        cols = slice(half * 4 * CH, (half + 1) * 4 * CH)
        block = (jnp.transpose(dqt[h, :, cols]) * 0.125).astype(BF16)
        for t in range(4):
            piece = block[t * CH : (t + 1) * CH]
            dq16[h, 4 * half + t] = jnp.concatenate([piece[:PK], piece[PK:]], axis=1)
        start([q_copy(h, d) for d, slot in Z_SLOT.items() if d and slot // 4 == half])

    def kc_copy(h):
        return remote(dkv16.at[h], r_core.at[h], kc_send.at[h], kc_recv.at[h], dev(other=True))

    def send_core(h):
        dkv16[h] = dkv[h, HALF:].astype(BF16)
        kc_copy(h).start()

    def kx_copy(h, d):
        slot = X_SLOT[d]
        back = X_SLOT[2 if d == 2 else -d]
        return remote(
            x16.at[h, pl.ds((slot - 1) * CH, CH)], r_x.at[h, back - 1], kx_send.at[h, slot],
            kx_recv.at[h, slot], dev(dx=d),
        )

    def send_x(h):
        kc_copy(h).wait_recv()
        total = dkv[h, :HALF] + r_core[h].astype(F32)
        x16[h] = total[CH:].astype(BF16)
        start([kx_copy(h, d) for d in X_SLOT if d])
        dkv[h, :CH] = total[:CH]

    lane = lax.broadcasted_iota(jnp.int32, (HALF, 2 * D), 1)

    @pl.loop(0, 4 * HL)
    def _(t):
        h = (t + 2) % HL
        late = jnp.where((t >= 4) & (t < 10), 1, 0)
        sib = jnp.where((t >= 1) & (t < 7), 1, 0)

        @pl.when(t == 1)
        def _():
            arrive([c_copy(i) for i in range(8)])

        @pl.when(t == 2)
        def _():
            for r in range(NY):
                for sign in (1, -1):
                    z_copy(3, sign, r).wait_recv()
                    if r in halves(4, 4, sign):
                        z_copy(4, sign, r).start()
            arrive([s_copy(3, 1), s_copy(3, -1)])
            s_copy(4, 1).start()

        @pl.when(t == 4)
        def _():
            arrive([z_copy(4, sign, r) for sign in (1, -1) for r in halves(4, 4, sign)])
            s_copy(4, 1).wait_recv()
            join(range(4, 8))
            send_dq(2, 0)

        cols = pl.ds(pl.multiple_of(late * (4 * CH), 4 * CH), 4 * CH)
        js = pl.ds(pl.multiple_of(sib * HALF, HALF), HALF)
        norms = stat_all[pl.ds(h, 1), cols]
        dels = stat_all[pl.ds(8 + h, 1), cols]
        rows_q = qg[h, cols]
        both = kv[h, js]
        zero = jnp.zeros_like(both)
        scores = nt(jnp.where(lane < D, both, zero), rows_q)
        dweights = nt(jnp.where(lane < D, zero, both), rows_q)
        weights = jnp.exp(scores - norms)
        dscores = (weights * (dweights - dels)).astype(BF16)
        low = weights.astype(BF16)
        dkv[h, js] += jnp.where(lane < D, nn(dscores, rows_q), nn(low, rows_q))
        dqt[h, :, cols] += tn(both, dscores)[:D]

        @pl.when((t >= 4) & (t < 7))
        def _():
            send_core(h)

        @pl.when((t >= 7) & (t < 10))
        def _():
            send_dq(h, 1)

        @pl.when(t >= 9)
        def _():
            send_x(h)

        @pl.when(t >= 10)
        def _():
            send_dq(h, 0)

    def fkv_copy(h, r):
        return remote(
            fin_kv.at[h, pl.ds(r * SUB, SUB)], r_kv.at[h, y], f_send.at[h, r], f_recv.at[h, r],
            dev(dy=r),
        )

    def fq_copy(r):
        return remote(fin_q.at[r], r_fq.at[y], f_send.at[HL, r], f_recv.at[HL, r], dev(dy=r))

    for h in (2, 0, 1):
        arrive([kx_copy(h, d) for d in X_SLOT if d])
        total = dkv[h, :CH]
        for slot in range(NX - 1):
            total = total + r_x[h, slot].astype(F32)
        total = total.astype(BF16)
        fin_kv[h] = total
        start([fkv_copy(h, r) for r in order])
        r_kv[h, y] = total[:SUB]
    for h in range(HL):
        arrive([q_copy(h, d) for d in Z_SLOT if d])
        total = dq16[h, 0].astype(F32)
        for slot in range(1, NZ):
            total = total + r_q[h, slot].astype(F32)
        total = total.astype(BF16)
        for r in range(NY):
            at = (r % 2) * SUB
            side = (r // 2) * D
            fin_q[r, :, h * D : (h + 1) * D] = total[at : at + SUB, side : side + D]
    start([fq_copy(r) for r in order])
    r_fq[y] = fin_q[0]
    arrive([fkv_copy(h, r) for h in range(HL) for r in order] + [fq_copy(r) for r in order])
    out_kv[...] = r_kv[...]
    out_q[...] = r_fq[...]

    done = [y_copy(r, kind) for r in order for kind in range(3)]
    for step in range(1, NZ // 2 + 1):
        for sign in (1, -1):
            done += [z_copy(step, sign, r) for r in halves(step, NZ // 2, sign)]
            if step < NZ // 2 or sign > 0:
                done.append(s_copy(step, sign))
    for step in range(1, NX // 2 + 1):
        for sign in (1, -1):
            done += [x_copy(step, sign, r) for r in halves(step, NX // 2, sign)]
    done += [c_copy(i) for i in range(8)] + [kc_copy(h) for h in range(HL)]
    done += [kx_copy(h, d) for h in range(HL) for d in X_SLOT if d]
    done += [q_copy(h, d) for h in range(HL) for d in Z_SLOT if d]
    done += [fkv_copy(h, r) for h in range(HL) for r in order] + [fq_copy(r) for r in order]
    for copy in done:
        copy.wait_send()
    for score in range(2):

        @pl.when(jnp.logical_not(lse_local(score)))
        def _():
            lse_copy(score).wait_send()


def place(kv_ref, q_ref, dq_ref, dk_ref, dv_ref):
    for n in range(NY):
        for h in range(HL):
            cols = slice((n * HL + h) * D, (n * HL + h + 1) * D)
            pair = kv_ref[h, n]
            dk_ref[:, cols] = pair[:, :D]
            dv_ref[:, cols] = pair[:, D:]
        dq_ref[:, n * HL * D : (n + 1) * HL * D] = q_ref[n]


def local(queries, keys, values, attended, grad_out, logsumexp):
    dma = pltpu.SemaphoreType.DMA
    vm = pltpu.VMEM
    whole = pl.BlockSpec(memory_space=pltpu.VMEM)
    sums = pl.pallas_call(
        kernel,
        out_shape=(
            jax.ShapeDtypeStruct((HL, NY, SUB, 2 * D), BF16),
            jax.ShapeDtypeStruct((NY, SUB, HL * D), BF16),
        ),
        in_specs=[whole] * 6,
        out_specs=[whole] * 2,
        scratch_shapes=[
            vm((NY, HL, SUB, 2 * D), BF16),
            vm((NY, HL, SUB, 2 * D), BF16),
            vm((NY, 8, SUB), F32),
            vm((2, 2, 8, SUB), F32),
            vm((HL, NI, 2 * D), BF16),
            vm((HL, NJ, 2 * D), BF16),
            vm((2, 2, 8, SUB), F32),
            vm((NY, 8, SUB), F32),
            vm((NZ, 16, CH), F32),
            vm((16, NI), F32),
            vm((HL, D, NI), F32),
            vm((HL, NJ, 2 * D), F32),
            vm((HL, HALF, 2 * D), BF16),
            vm((HL, HALF, 2 * D), BF16),
            vm((HL, HALF - CH, 2 * D), BF16),
            vm((HL, NX - 1, CH, 2 * D), BF16),
            vm((HL, NZ, PK, 2 * D), BF16),
            vm((HL, NZ, PK, 2 * D), BF16),
            vm((HL, CH, 2 * D), BF16),
            vm((NY, SUB, HL * D), BF16),
            vm((HL, NY, SUB, 2 * D), BF16),
            vm((NY, SUB, HL * D), BF16),
            dma((NY, 3)), dma((NY, 3)),
            dma((2,)), dma((2,)),
            dma((2, NZ // 2 + 1, NY)), dma((2, NZ // 2 + 1, NY)),
            dma((2, NZ // 2 + 1)), dma((2, NZ // 2 + 1)),
            dma((2, NX // 2 + 1, NY)), dma((2, NX // 2 + 1, NY)),
            dma((8,)), dma((8,)),
            dma((HL,)), dma((HL,)),
            dma((HL, NX)), dma((HL, NX)),
            dma((HL, NZ)), dma((HL, NZ)),
            dma((HL + 1, NY)), dma((HL + 1, NY)),
        ],
        compiler_params=pltpu.CompilerParams(
            collective_id=0, has_side_effects=True, vmem_limit_bytes=56 << 20
        ),
        name="attention_grad",
    )(queries, keys, values, attended, grad_out, jnp.transpose(logsumexp))
    out = jax.ShapeDtypeStruct(queries.shape, BF16)
    return pl.pallas_call(
        place, out_shape=(out, out, out), in_specs=[whole] * 2, out_specs=[whole] * 3, name="place"
    )(*sums)


def solution(mesh):
    rows = P(("ctx", "head"), None)
    return jax.shard_map(
        local,
        mesh=mesh,
        in_specs=(rows,) * 5 + (P("ctx", "head"),),
        out_specs=(rows,) * 3,
        check_vma=False,
    )
```

time: 1370 us -> 61.7 us (0.05)
  the two profiles are of different devices: /device:TPU:1 before, /device:TPU:8 now
where the time goes in v2:
time: 61.7 us; the launch traced here: 61.5 us
  Pallas kernels  60.9 us (99%)
  between operations  0.64 us (1%)
    pallas_call x1, Pallas kernels, local(): pl.pallas_call(kernel, out_shape=(jax.ShapeDtypeStruct((HL, NY, SUB, 2 *...  59.1 us
    pallas_call x1, Pallas kernels, local(): pl.pallas_call(place, out_shape=(out, out, out), in_specs=[whole] * 2, ou...  1.78 us

profile of v2, /device:TPU:8, one launch (start us, length us, event | category | flops | bytes accessed | tf_op | source)
XLA Modules:
  0.0 61.5 jit_solution(3087039185966430759)
XLA Ops:
  0.6 59.1 %attention_grad.1 = (bf16[3,4,48,128]{3,2,1,0:T(8,128)(2,1)}, bf16[4,48,192]{2,1,0:T(8,128)(2,1)}) custom-call(bf16[48,768]{1,0:T(8,128)(2,1)} %q_ref.1, bf16[48,768]{1,0:T(8,128)(2,1)} %k_ref.1, bf16[48,768]{1,0:T(8,128)(2,1)} %v_ref.1, bf16[48,768]{1,0:T(8,128)(2,1)} %o_ref.1, bf16[48,768]{1,0:T(8,128)(2,1)} %g_ref.1, f32[3,192]{1,0:T(4,128)} %bitcast.1), custom_call_target="tpu_custom_call" | custom-call | tf_op jit(solution)/shard_map/attention_grad/pallas_call | solution.py:397
  59.7 1.8 %place.1 = (bf16[48,768]{1,0:T(8,128)(2,1)}, bf16[48,768]{1,0:T(8,128)(2,1)}, bf16[48,768]{1,0:T(8,128)(2,1)}) custom-call(bf16[3,4,48,128]{3,2,1,0:T(8,128)(2,1)} %get-tuple-element.5.kv_ref, bf16[4,48,192]{2,1,0:T(8,128)(2,1)} %get-tuple-element.6.q_ref), custom_call_target="tpu_custom_call" | custom-call | tf_op jit(solution)/shard_map/place/pallas_call | solution.py:445

commit v3 on v2

--- a/solution.py
+++ b/solution.py
@@ -21,6 +21,7 @@
 HALF = NJ // 2
 Z_SLOT = {0: 0, 1: 1, -1: 2, 2: 3, -2: 4, 3: 5, -3: 6, 4: 7}
 X_SLOT = {0: 0, 1: 1, -1: 2, 2: 3}
+NC = NY + 2 * (NX - 1)
 PK = CH // 2
 
 
@@ -39,9 +40,9 @@
 def kernel(
     q_ref, k_ref, v_ref, o_ref, g_ref, lse_ref, out_kv, out_q,
     st_qg, st_kv, st_d, st_lse, qg, kv, r_lse, r_d, stat, stat_all, dqt, dkv, dkv16, r_core, x16,
-    r_x, dq16, r_q, fin_kv, fin_q, r_kv, r_fq,
+    r_x, dq32, dq16, r_v, r_q, fin_kv, fin_q, r_kv, r_fq,
     a_send, a_recv, l_send, l_recv, z_send, z_recv, s_send, s_recv, x_send, x_recv, c_send, c_recv,
-    kc_send, kc_recv, kx_send, kx_recv, q_send, q_recv, f_send, f_recv,
+    kc_send, kc_recv, kx_send, kx_recv, v_send, v_recv, q_send, q_recv, f_send, f_recv,
 ):
     c = lax.axis_index("ctx")
     g = lax.axis_index("head")
@@ -73,7 +74,7 @@
 
     barrier = pltpu.get_barrier_semaphore()
     peers = [dev(dy=dy, other=o) for dy in range(NY) for o in (False, True) if dy or o]
-    peers += [dev(dz=d) for d in Z_SLOT if d] + [dev(dx=d) for d in X_SLOT if d]
+    peers += [dev(dz=d) for d in (1, -1, 2, -2)] + [dev(dx=d) for d in X_SLOT if d]
     for peer in peers:
         pl.semaphore_signal(barrier, inc=1, device_id=peer, device_id_type=MESH)
 
@@ -84,24 +85,28 @@
         dst = (qg.at[:, rows], kv.at[:, rows], r_d.at[NY - r])[kind]
         return remote(src, dst, a_send.at[r, kind], a_recv.at[r, kind], dev(dy=r))
 
-    def ring(buf, slots, axis, last, step, sign, r, send, recv):
+    def z_copy(step, sign, r):
         d = -sign * (step - 1)
-        a = slots[d]
-        b = slots[last if step == last else d - sign]
+        a = Z_SLOT[d]
+        b = Z_SLOT[4 if step == NZ // 2 else d - sign]
         way = 0 if sign > 0 else 1
         return remote(
-            buf.at[:, pl.ds(a * CH + r * SUB, SUB)], buf.at[:, pl.ds(b * CH + r * SUB, SUB)],
-            send.at[way, step, r], recv.at[way, step, r], dev(**{axis: sign}),
-        )
-
-    def z_copy(step, sign, r):
-        return ring(qg, Z_SLOT, "dz", NZ // 2, step, sign, r, z_send, z_recv)
-
-    def x_copy(step, sign, r):
-        return ring(kv, X_SLOT, "dx", NX // 2, step, sign, r, x_send, x_recv)
-
-    def halves(step, last, sign):
-        return range(NY) if step < last else ((0, 1) if sign > 0 else (2, 3))
+            qg.at[:, pl.ds(a * CH + r * SUB, SUB)], qg.at[:, pl.ds(b * CH + r * SUB, SUB)],
+            z_send.at[way, step, r], z_recv.at[way, step, r], dev(dz=sign),
+        )
+
+    def x_copy(d, r):
+        back = X_SLOT[2 if d == 2 else -d]
+        return remote(
+            kv.at[:, pl.ds(r * SUB, SUB)], kv.at[:, pl.ds(back * CH + r * SUB, SUB)],
+            x_send.at[X_SLOT[d], r], x_recv.at[X_SLOT[d], r], dev(dx=d),
+        )
+
+    def x_copies(r):
+        return [x_copy(d, r) for d in (2, 1, -1)]
+
+    def parts(step, sign):
+        return range(NY) if step < NZ // 2 else ((0, 1) if sign > 0 else (2, 3))
 
     def s_copy(step, sign):
         d = -sign * (step - 1)
@@ -112,9 +117,10 @@
         )
 
     def c_copy(i):
-        begin, rows = [(r * SUB, SUB) for r in range(NY)][i] if i < NY else (
-            ((i - 3) * CH, CH) if i < 6 else (3 * CH + (i - 6) * (CH // 2), CH // 2)
-        )
+        if i < NY:
+            begin, rows = i * SUB, SUB
+        else:
+            begin, rows = CH + ((i - NY) // 2) * CH + (i % 2) * (CH // 2), CH // 2
         return remote(
             kv.at[:, pl.ds(begin, rows)], kv.at[:, pl.ds(HALF + begin, rows)],
             c_send.at[i], c_recv.at[i], dev(other=True),
@@ -142,7 +148,7 @@
     pl.semaphore_wait(barrier, len(peers))
     start([y_copy(r, 1) for r in order])
     kv[:, 0:SUB] = st_kv[y]
-    start([x_copy(1, 1, 0), x_copy(1, -1, 0), c_copy(0)])
+    start(x_copies(0) + [c_copy(0)])
     gs = g_ref[...]
     stage(st_qg, q_ref[...] * jnp.asarray(0.125, BF16), gs)
     start([y_copy(r, 0) for r in order])
@@ -179,7 +185,7 @@
     for r, kind in ((1, 1), (3, 1), (1, 0), (3, 0), (2, 1), (2, 0)):
         y_copy(NY - r, kind).wait_recv()
         if kind == 1:
-            start([x_copy(1, 1, r), x_copy(1, -1, r), c_copy(r)])
+            start(x_copies(r) + [c_copy(r)])
         else:
             start([z_copy(1, 1, r), z_copy(1, -1, r)])
     for r in range(1, NY):
@@ -198,21 +204,16 @@
         stat[0, 0:8, r * SUB : (r + 1) * SUB] = r_lse[from_at % 2, from_at // 2]
         stat[0, 8:16, r * SUB : (r + 1) * SUB] = r_d[r]
     start([s_copy(1, 1), s_copy(1, -1)])
-    for r in (0, 1, 3, 2):
-        for sign in (1, -1):
-            x_copy(1, sign, r).wait_recv()
-            if r in halves(2, 2, sign):
-                x_copy(2, sign, r).start()
+    for i, r in enumerate((0, 1, 3, 2)):
+        arrive(x_copies(r))
+        if i % 2:
+            start([c_copy(NY + 2 * n + i // 2) for n in range(NX - 1)])
         for sign in (1, -1):
             z_copy(1, sign, r).wait_recv()
             z_copy(2, sign, r).start()
-    start([c_copy(4), c_copy(5)])
     for sign in (1, -1):
         s_copy(1, sign).wait_recv()
         s_copy(2, sign).start()
-    for sign, i in ((1, 6), (-1, 7)):
-        arrive([x_copy(2, sign, r) for r in halves(2, 2, sign)])
-        c_copy(i).start()
     for r in (0, 1, 3, 2):
         for sign in (1, -1):
             z_copy(2, sign, r).wait_recv()
@@ -227,20 +228,43 @@
 
     join(range(4))
 
+    def v_copy(h, i):
+        slot = (5, 6, 7, 7)[i]
+        rows = pl.ds((0, 0, 0, PK // 2)[i], (PK, PK, PK // 2, PK // 2)[i])
+        return remote(
+            dq16.at[h, slot, rows], r_v.at[h, i, rows], v_send.at[h, i], v_recv.at[h, i],
+            dev(dz=(2, -2, 2, -2)[i]),
+        )
+
     def q_copy(h, d):
         slot = Z_SLOT[d]
-        back = Z_SLOT[4 if d == 4 else -d]
+        back = Z_SLOT[-d]
         return remote(
             dq16.at[h, slot], r_q.at[h, back], q_send.at[h, slot], q_recv.at[h, slot], dev(dz=d)
         )
 
-    def send_dq(h, half):
+    def pack_dq(h, half):
         cols = slice(half * 4 * CH, (half + 1) * 4 * CH)
-        block = (jnp.transpose(dqt[h, :, cols]) * 0.125).astype(BF16)
+        block = jnp.transpose(dqt[h, :, cols]) * 0.125
         for t in range(4):
             piece = block[t * CH : (t + 1) * CH]
-            dq16[h, 4 * half + t] = jnp.concatenate([piece[:PK], piece[PK:]], axis=1)
-        start([q_copy(h, d) for d, slot in Z_SLOT.items() if d and slot // 4 == half])
+            dq32[h, 4 * half + t] = jnp.concatenate([piece[:PK], piece[PK:]], axis=1)
+
+    def send_far(h):
+        for slot in (5, 6, 7):
+            dq16[h, slot] = dq32[h, slot].astype(BF16)
+        start([v_copy(h, i) for i in range(4)])
+
+    def send_near(h):
+        arrive([v_copy(h, i) for i in range(4)])
+        half = PK // 2
+        dq16[h, 1] = (dq32[h, 1] + r_v[h, 0].astype(F32)).astype(BF16)
+        dq16[h, 2] = (dq32[h, 2] + r_v[h, 1].astype(F32)).astype(BF16)
+        dq16[h, 3, :half] = (dq32[h, 3, :half] + r_v[h, 2, :half].astype(F32)).astype(BF16)
+        dq16[h, 3, half:] = dq32[h, 3, half:].astype(BF16)
+        dq16[h, 4, :half] = dq32[h, 4, :half].astype(BF16)
+        dq16[h, 4, half:] = (dq32[h, 4, half:] + r_v[h, 3, half:].astype(F32)).astype(BF16)
+        start([q_copy(h, d) for d in (2, -2, 1, -1)])
 
     def kc_copy(h):
         return remote(dkv16.at[h], r_core.at[h], kc_send.at[h], kc_recv.at[h], dev(other=True))
@@ -268,30 +292,30 @@
 
     @pl.loop(0, 4 * HL)
     def _(t):
-        h = (t + 2) % HL
+        h = jnp.where((t >= 7) & (t < 10), t + 1, t + 2) % HL
         late = jnp.where((t >= 4) & (t < 10), 1, 0)
         sib = jnp.where((t >= 1) & (t < 7), 1, 0)
 
         @pl.when(t == 1)
         def _():
-            arrive([c_copy(i) for i in range(8)])
+            arrive([c_copy(i) for i in range(NC)])
 
         @pl.when(t == 2)
         def _():
             for r in range(NY):
                 for sign in (1, -1):
                     z_copy(3, sign, r).wait_recv()
-                    if r in halves(4, 4, sign):
+                    if r in parts(4, sign):
                         z_copy(4, sign, r).start()
             arrive([s_copy(3, 1), s_copy(3, -1)])
             s_copy(4, 1).start()
 
         @pl.when(t == 4)
         def _():
-            arrive([z_copy(4, sign, r) for sign in (1, -1) for r in halves(4, 4, sign)])
+            arrive([z_copy(4, sign, r) for sign in (1, -1) for r in parts(4, sign)])
             s_copy(4, 1).wait_recv()
             join(range(4, 8))
-            send_dq(2, 0)
+            pack_dq(2, 0)
 
         cols = pl.ds(pl.multiple_of(late * (4 * CH), 4 * CH), 4 * CH)
         js = pl.ds(pl.multiple_of(sib * HALF, HALF), HALF)
@@ -314,15 +338,24 @@
 
         @pl.when((t >= 7) & (t < 10))
         def _():
-            send_dq(h, 1)
-
-        @pl.when(t >= 9)
+            pack_dq(h, 1)
+            send_far(h)
+
+        @pl.when(t == 7)
+        def _():
+            send_x(2)
+
+        @pl.when(t >= 10)
         def _():
             send_x(h)
-
-        @pl.when(t >= 10)
-        def _():
-            send_dq(h, 0)
+            pack_dq(h, 0)
+
+        @pl.when(t == 10)
+        def _():
+            send_near(2)
+
+    send_near(0)
+    send_near(1)
 
     def fkv_copy(h, r):
         return remote(
@@ -342,10 +375,10 @@
         fin_kv[h] = total
         start([fkv_copy(h, r) for r in order])
         r_kv[h, y] = total[:SUB]
-    for h in range(HL):
-        arrive([q_copy(h, d) for d in Z_SLOT if d])
-        total = dq16[h, 0].astype(F32)
-        for slot in range(1, NZ):
+    for h in (2, 0, 1):
+        arrive([q_copy(h, d) for d in (2, -2, 1, -1)])
+        total = dq32[h, 0]
+        for slot in range(1, 5):
             total = total + r_q[h, slot].astype(F32)
         total = total.astype(BF16)
         for r in range(NY):
@@ -361,15 +394,14 @@
     done = [y_copy(r, kind) for r in order for kind in range(3)]
     for step in range(1, NZ // 2 + 1):
         for sign in (1, -1):
-            done += [z_copy(step, sign, r) for r in halves(step, NZ // 2, sign)]
+            done += [z_copy(step, sign, r) for r in parts(step, sign)]
             if step < NZ // 2 or sign > 0:
                 done.append(s_copy(step, sign))
-    for step in range(1, NX // 2 + 1):
-        for sign in (1, -1):
-            done += [x_copy(step, sign, r) for r in halves(step, NX // 2, sign)]
-    done += [c_copy(i) for i in range(8)] + [kc_copy(h) for h in range(HL)]
+    done += [copy for r in range(NY) for copy in x_copies(r)]
+    done += [c_copy(i) for i in range(NC)] + [kc_copy(h) for h in range(HL)]
     done += [kx_copy(h, d) for h in range(HL) for d in X_SLOT if d]
-    done += [q_copy(h, d) for h in range(HL) for d in Z_SLOT if d]
+    done += [q_copy(h, d) for h in range(HL) for d in (2, -2, 1, -1)]
+    done += [v_copy(h, i) for h in range(HL) for i in range(4)]
     done += [fkv_copy(h, r) for h in range(HL) for r in order] + [fq_copy(r) for r in order]
     for copy in done:
         copy.wait_send()
@@ -419,8 +451,10 @@
             vm((HL, HALF, 2 * D), BF16),
             vm((HL, HALF - CH, 2 * D), BF16),
             vm((HL, NX - 1, CH, 2 * D), BF16),
+            vm((HL, NZ, PK, 2 * D), F32),
             vm((HL, NZ, PK, 2 * D), BF16),
-            vm((HL, NZ, PK, 2 * D), BF16),
+            vm((HL, 4, PK, 2 * D), BF16),
+            vm((HL, 5, PK, 2 * D), BF16),
             vm((HL, CH, 2 * D), BF16),
             vm((NY, SUB, HL * D), BF16),
             vm((HL, NY, SUB, 2 * D), BF16),
@@ -429,11 +463,12 @@
             dma((2,)), dma((2,)),
             dma((2, NZ // 2 + 1, NY)), dma((2, NZ // 2 + 1, NY)),
             dma((2, NZ // 2 + 1)), dma((2, NZ // 2 + 1)),
-            dma((2, NX // 2 + 1, NY)), dma((2, NX // 2 + 1, NY)),
-            dma((8,)), dma((8,)),
+            dma((NX, NY)), dma((NX, NY)),
+            dma((NC,)), dma((NC,)),
             dma((HL,)), dma((HL,)),
             dma((HL, NX)), dma((HL, NX)),
-            dma((HL, NZ)), dma((HL, NZ)),
+            dma((HL, 4)), dma((HL, 4)),
+            dma((HL, 5)), dma((HL, 5)),
             dma((HL + 1, NY)), dma((HL + 1, NY)),
         ],
         compiler_params=pltpu.CompilerParams(

time: 61.7 us -> 61 us (0.989)
  the two profiles are of different devices: /device:TPU:8 before, /device:TPU:1 now
where the time goes in v3:
time: 61 us; the launch traced here: 60.6 us
  Pallas kernels  59.9 us (98%)
  between operations  0.64 us (1%)
    pallas_call x1, Pallas kernels, local(): pl.pallas_call(kernel, out_shape=(jax.ShapeDtypeStruct((HL, NY, SUB, 2 *...  58.1 us
    pallas_call x1, Pallas kernels, local(): pl.pallas_call(place, out_shape=(out, out, out), in_specs=[whole] * 2, ou...  1.78 us

profile of v3, /device:TPU:1, one launch (start us, length us, event | category | flops | bytes accessed | tf_op | source)
XLA Modules:
  0.0 60.6 jit_solution(13167624774005898353)
XLA Ops:
  0.6 58.1 %attention_grad.1 = (bf16[3,4,48,128]{3,2,1,0:T(8,128)(2,1)}, bf16[4,48,192]{2,1,0:T(8,128)(2,1)}) custom-call(bf16[48,768]{1,0:T(8,128)(2,1)} %q_ref.1, bf16[48,768]{1,0:T(8,128)(2,1)} %k_ref.1, bf16[48,768]{1,0:T(8,128)(2,1)} %v_ref.1, bf16[48,768]{1,0:T(8,128)(2,1)} %o_ref.1, bf16[48,768]{1,0:T(8,128)(2,1)} %g_ref.1, f32[3,192]{1,0:T(4,128)} %bitcast.1), custom_call_target="tpu_custom_call" | custom-call | tf_op jit(solution)/shard_map/attention_grad/pallas_call | solution.py:429
  58.8 1.8 %place.1 = (bf16[48,768]{1,0:T(8,128)(2,1)}, bf16[48,768]{1,0:T(8,128)(2,1)}, bf16[48,768]{1,0:T(8,128)(2,1)}) custom-call(bf16[3,4,48,128]{3,2,1,0:T(8,128)(2,1)} %get-tuple-element.5.kv_ref, bf16[4,48,192]{2,1,0:T(8,128)(2,1)} %get-tuple-element.6.q_ref), custom_call_target="tpu_custom_call" | custom-call | tf_op jit(solution)/shard_map/place/pallas_call | solution.py:480

commit v4 on v3

--- a/solution.py
+++ b/solution.py
@@ -288,20 +288,48 @@
         start([kx_copy(h, d) for d in X_SLOT if d])
         dkv[h, :CH] = total[:CH]
 
+    def fkv_copy(h, r):
+        return remote(
+            fin_kv.at[h, pl.ds(r * SUB, SUB)], r_kv.at[h, y], f_send.at[h, r], f_recv.at[h, r],
+            dev(dy=r),
+        )
+
+    def fq_copy(r):
+        return remote(fin_q.at[r], r_fq.at[y], f_send.at[HL, r], f_recv.at[HL, r], dev(dy=r))
+
+    def finish_kv(h):
+        arrive([kx_copy(h, d) for d in X_SLOT if d])
+        total = dkv[h, :CH]
+        for slot in range(NX - 1):
+            total = total + r_x[h, slot].astype(F32)
+        total = total.astype(BF16)
+        fin_kv[h] = total
+        start([fkv_copy(h, r) for r in order])
+        r_kv[h, y] = total[:SUB]
+
+    def finish_q(h):
+        arrive([q_copy(h, d) for d in (2, -2, 1, -1)])
+        total = dq32[h, 0]
+        for slot in range(1, 5):
+            total = total + r_q[h, slot].astype(F32)
+        total = total.astype(BF16)
+        for r in range(NY):
+            at = (r % 2) * SUB
+            side = (r // 2) * D
+            fin_q[r, :, h * D : (h + 1) * D] = total[at : at + SUB, side : side + D]
+
     lane = lax.broadcasted_iota(jnp.int32, (HALF, 2 * D), 1)
 
     @pl.loop(0, 4 * HL)
     def _(t):
-        h = jnp.where((t >= 7) & (t < 10), t + 1, t + 2) % HL
+        h = jnp.where(t < 4, t % 2, (t - 4) // 2)
+        h = jnp.where(t < 8, h, 2)
         late = jnp.where((t >= 4) & (t < 10), 1, 0)
-        sib = jnp.where((t >= 1) & (t < 7), 1, 0)
-
-        @pl.when(t == 1)
+        sib = jnp.where((t == 3) | ((t >= 2) & (t % 2 == 0)), 1, 0)
+
+        @pl.when(t == 2)
         def _():
             arrive([c_copy(i) for i in range(NC)])
-
-        @pl.when(t == 2)
-        def _():
             for r in range(NY):
                 for sign in (1, -1):
                     z_copy(3, sign, r).wait_recv()
@@ -315,7 +343,6 @@
             arrive([z_copy(4, sign, r) for sign in (1, -1) for r in parts(4, sign)])
             s_copy(4, 1).wait_recv()
             join(range(4, 8))
-            pack_dq(2, 0)
 
         cols = pl.ds(pl.multiple_of(late * (4 * CH), 4 * CH), 4 * CH)
         js = pl.ds(pl.multiple_of(sib * HALF, HALF), HALF)
@@ -332,59 +359,36 @@
         dkv[h, js] += jnp.where(lane < D, nn(dscores, rows_q), nn(low, rows_q))
         dqt[h, :, cols] += tn(both, dscores)[:D]
 
-        @pl.when((t >= 4) & (t < 7))
+        @pl.when((t == 2) | (t == 3) | (t == 11))
+        def _():
+            pack_dq(h, 0)
+
+        @pl.when((t == 4) | (t == 6) | (t == 10))
         def _():
             send_core(h)
 
-        @pl.when((t >= 7) & (t < 10))
+        @pl.when((t == 5) | (t == 7) | (t == 9))
         def _():
             pack_dq(h, 1)
             send_far(h)
 
-        @pl.when(t == 7)
-        def _():
-            send_x(2)
-
-        @pl.when(t >= 10)
+        @pl.when((t == 5) | (t == 7) | (t == 11))
         def _():
             send_x(h)
-            pack_dq(h, 0)
+
+        @pl.when((t == 8) | (t == 10))
+        def _():
+            send_near((t - 8) // 2)
+            finish_kv((t - 8) // 2)
 
         @pl.when(t == 10)
         def _():
-            send_near(2)
-
-    send_near(0)
-    send_near(1)
-
-    def fkv_copy(h, r):
-        return remote(
-            fin_kv.at[h, pl.ds(r * SUB, SUB)], r_kv.at[h, y], f_send.at[h, r], f_recv.at[h, r],
-            dev(dy=r),
-        )
-
-    def fq_copy(r):
-        return remote(fin_q.at[r], r_fq.at[y], f_send.at[HL, r], f_recv.at[HL, r], dev(dy=r))
-
-    for h in (2, 0, 1):
-        arrive([kx_copy(h, d) for d in X_SLOT if d])
-        total = dkv[h, :CH]
-        for slot in range(NX - 1):
-            total = total + r_x[h, slot].astype(F32)
-        total = total.astype(BF16)
-        fin_kv[h] = total
-        start([fkv_copy(h, r) for r in order])
-        r_kv[h, y] = total[:SUB]
-    for h in (2, 0, 1):
-        arrive([q_copy(h, d) for d in (2, -2, 1, -1)])
-        total = dq32[h, 0]
-        for slot in range(1, 5):
-            total = total + r_q[h, slot].astype(F32)
-        total = total.astype(BF16)
-        for r in range(NY):
-            at = (r % 2) * SUB
-            side = (r // 2) * D
-            fin_q[r, :, h * D : (h + 1) * D] = total[at : at + SUB, side : side + D]
+            finish_q(0)
+
+    send_near(2)
+    finish_q(1)
+    finish_kv(2)
+    finish_q(2)
     start([fq_copy(r) for r in order])
     r_fq[y] = fin_q[0]
     arrive([fkv_copy(h, r) for h in range(HL) for r in order] + [fq_copy(r) for r in order])
@@ -429,8 +433,8 @@
     sums = pl.pallas_call(
         kernel,
         out_shape=(
-            jax.ShapeDtypeStruct((HL, NY, SUB, 2 * D), BF16),
-            jax.ShapeDtypeStruct((NY, SUB, HL * D), BF16),
+            pltpu.VMEM((HL, NY, SUB, 2 * D), BF16),
+            pltpu.VMEM((NY, SUB, HL * D), BF16),
         ),
         in_specs=[whole] * 6,
         out_specs=[whole] * 2,
@@ -479,7 +483,7 @@
     out = jax.ShapeDtypeStruct(queries.shape, BF16)
     return pl.pallas_call(
         place, out_shape=(out, out, out), in_specs=[whole] * 2, out_specs=[whole] * 3, name="place"
-    )(*sums)
+    )(*[pltpu.with_memory_space_constraint(part, pltpu.VMEM) for part in sums])
 
 
 def solution(mesh):

time: 61 us -> 59.3 us (0.972)
  Pallas kernels: 59.9 us -> 57.7 us
    pallas_call x1, Pallas kernels: 58.1 us -> 56.9 us  [local(): pl.pallas_call(kernel, out_shape=(pltpu.VMEM((HL, NY, SUB, 2 * D), BF16),...]
    pallas_call x1, Pallas kernels: 1.78 us -> 0.81 us  [local(): pl.pallas_call(place, out_shape=(out, out, out), in_specs=[whole] * 2, ou...]
where the time goes in v4:
time: 59.3 us; the launch traced here: 58.3 us
  Pallas kernels  57.7 us (97%)
  between operations  0.64 us (1%)
    pallas_call x1, Pallas kernels, local(): pl.pallas_call(kernel, out_shape=(pltpu.VMEM((HL, NY, SUB, 2 * D), BF16),...  56.9 us

profile of v4, /device:TPU:1, one launch (start us, length us, event | category | flops | bytes accessed | tf_op | source)
XLA Modules:
  0.0 58.3 jit_solution(10900283629468597976)
XLA Ops:
  0.6 56.9 %attention_grad.1 = (bf16[3,4,48,128]{3,2,1,0:T(8,128)(2,1)S(1)}, bf16[4,48,192]{2,1,0:T(8,128)(2,1)S(1)}) custom-call(bf16[48,768]{1,0:T(8,128)(2,1)} %q_ref.1, bf16[48,768]{1,0:T(8,128)(2,1)} %k_ref.1, bf16[48,768]{1,0:T(8,128)(2,1)} %v_ref.1, bf16[48,768]{1,0:T(8,128)(2,1)} %o_ref.1, bf16[48,768]{1,0:T(8,128)(2,1)} %g_ref.1, f32[3,192]{1,0:T(4,128)} %bitcast.1), custom_call_target="tpu_custom_call" | custom-call | tf_op jit(solution)/shard_map/attention_grad/pallas_call | solution.py:433
  57.5 0.8 %place.1 = (bf16[48,768]{1,0:T(8,128)(2,1)}, bf16[48,768]{1,0:T(8,128)(2,1)}, bf16[48,768]{1,0:T(8,128)(2,1)}) custom-call(bf16[3,4,48,128]{3,2,1,0:T(8,128)(2,1)S(1)} %get-tuple-element.5.kv_ref, bf16[4,48,192]{2,1,0:T(8,128)(2,1)S(1)} %get-tuple-element.6.q_ref), custom_call_target="tpu_custom_call" | custom-call | tf_op jit(solution)/shard_map/place/pallas_call | solution.py:484

commit v5 on v4

--- a/solution.py
+++ b/solution.py
@@ -22,6 +22,7 @@
 Z_SLOT = {0: 0, 1: 1, -1: 2, 2: 3, -2: 4, 3: 5, -3: 6, 4: 7}
 X_SLOT = {0: 0, 1: 1, -1: 2, 2: 3}
 NC = NY + 2 * (NX - 1)
+HS = SUB // 2
 PK = CH // 2
 
 
@@ -40,9 +41,10 @@
 def kernel(
     q_ref, k_ref, v_ref, o_ref, g_ref, lse_ref, out_kv, out_q,
     st_qg, st_kv, st_d, st_lse, qg, kv, r_lse, r_d, stat, stat_all, dqt, dkv, dkv16, r_core, x16,
-    r_x, dq32, dq16, r_v, r_q, fin_kv, fin_q, r_kv, r_fq,
+    r_x, dq32, dq16, r_v, r_q, fin_kv, fin_q, r_kv, r_fq, last_kv, r_lkv, last_q, r_lq,
     a_send, a_recv, l_send, l_recv, z_send, z_recv, s_send, s_recv, x_send, x_recv, c_send, c_recv,
     kc_send, kc_recv, kx_send, kx_recv, v_send, v_recv, q_send, q_recv, f_send, f_recv,
+    lx_send, lx_recv, lq_send, lq_recv,
 ):
     c = lax.axis_index("ctx")
     g = lax.axis_index("head")
@@ -247,15 +249,18 @@
         cols = slice(half * 4 * CH, (half + 1) * 4 * CH)
         block = jnp.transpose(dqt[h, :, cols]) * 0.125
         for t in range(4):
-            piece = block[t * CH : (t + 1) * CH]
-            dq32[h, 4 * half + t] = jnp.concatenate([piece[:PK], piece[PK:]], axis=1)
+            for r in range(NY):
+                at = t * CH + r * SUB
+                dq32[h, 4 * half + t, r * HS : (r + 1) * HS] = jnp.concatenate(
+                    [block[at : at + HS], block[at + HS : at + SUB]], axis=1
+                )
 
     def send_far(h):
         for slot in (5, 6, 7):
             dq16[h, slot] = dq32[h, slot].astype(BF16)
         start([v_copy(h, i) for i in range(4)])
 
-    def send_near(h):
+    def add_near(h):
         arrive([v_copy(h, i) for i in range(4)])
         half = PK // 2
         dq16[h, 1] = (dq32[h, 1] + r_v[h, 0].astype(F32)).astype(BF16)
@@ -264,7 +269,31 @@
         dq16[h, 3, half:] = dq32[h, 3, half:].astype(BF16)
         dq16[h, 4, :half] = dq32[h, 4, :half].astype(BF16)
         dq16[h, 4, half:] = (dq32[h, 4, half:] + r_v[h, 3, half:].astype(F32)).astype(BF16)
+
+    def send_near(h):
+        add_near(h)
         start([q_copy(h, d) for d in (2, -2, 1, -1)])
+
+    NEAR = (2, -2, 1, -1, 0)
+    FAR_X = (2, 1, -1, 0)
+
+    def lq_copy(d, r):
+        slot = Z_SLOT[d]
+        return remote(
+            last_q.at[slot, r], r_lq.at[y, Z_SLOT[-d]], lq_send.at[slot, r], lq_recv.at[slot, r],
+            dev(dz=d, dy=r),
+        )
+
+    def lx_copy(d, r):
+        slot = X_SLOT[d]
+        back = X_SLOT[2 if d == 2 else -d]
+        return remote(
+            last_kv.at[pl.ds(slot * CH + r * SUB, SUB)], r_lkv.at[y, back], lx_send.at[slot, r],
+            lx_recv.at[slot, r], dev(dx=d, dy=r),
+        )
+
+    last_x = [lx_copy(d, r) for r in (2, 1, 3, 0) for d in FAR_X if d or r]
+    last_z = [lq_copy(d, r) for r in (2, 1, 3, 0) for d in NEAR if d or r]
 
     def kc_copy(h):
         return remote(dkv16.at[h], r_core.at[h], kc_send.at[h], kc_recv.at[h], dev(other=True))
@@ -281,9 +310,12 @@
             kx_recv.at[h, slot], dev(dx=d),
         )
 
+    def all_cores(h):
+        kc_copy(h).wait_recv()
+        return dkv[h, :HALF] + r_core[h].astype(F32)
+
     def send_x(h):
-        kc_copy(h).wait_recv()
-        total = dkv[h, :HALF] + r_core[h].astype(F32)
+        total = all_cores(h)
         x16[h] = total[CH:].astype(BF16)
         start([kx_copy(h, d) for d in X_SLOT if d])
         dkv[h, :CH] = total[:CH]
@@ -295,7 +327,7 @@
         )
 
     def fq_copy(r):
-        return remote(fin_q.at[r], r_fq.at[y], f_send.at[HL, r], f_recv.at[HL, r], dev(dy=r))
+        return remote(fin_q.at[r], r_fq.at[y], f_send.at[HL - 1, r], f_recv.at[HL - 1, r], dev(dy=r))
 
     def finish_kv(h):
         arrive([kx_copy(h, d) for d in X_SLOT if d])
@@ -307,16 +339,16 @@
         start([fkv_copy(h, r) for r in order])
         r_kv[h, y] = total[:SUB]
 
+    def unpack(rows):
+        return jnp.concatenate([rows[:, :D], rows[:, D:]], axis=0).astype(BF16)
+
     def finish_q(h):
         arrive([q_copy(h, d) for d in (2, -2, 1, -1)])
         total = dq32[h, 0]
         for slot in range(1, 5):
             total = total + r_q[h, slot].astype(F32)
-        total = total.astype(BF16)
         for r in range(NY):
-            at = (r % 2) * SUB
-            side = (r // 2) * D
-            fin_q[r, :, h * D : (h + 1) * D] = total[at : at + SUB, side : side + D]
+            fin_q[r, :, h * D : (h + 1) * D] = unpack(total[r * HS : (r + 1) * HS])
 
     lane = lax.broadcasted_iota(jnp.int32, (HALF, 2 * D), 1)
 
@@ -359,7 +391,7 @@
         dkv[h, js] += jnp.where(lane < D, nn(dscores, rows_q), nn(low, rows_q))
         dqt[h, :, cols] += tn(both, dscores)[:D]
 
-        @pl.when((t == 2) | (t == 3) | (t == 11))
+        @pl.when((t == 2) | (t == 3))
         def _():
             pack_dq(h, 0)
 
@@ -372,7 +404,7 @@
             pack_dq(h, 1)
             send_far(h)
 
-        @pl.when((t == 5) | (t == 7) | (t == 11))
+        @pl.when((t == 5) | (t == 7))
         def _():
             send_x(h)
 
@@ -385,15 +417,38 @@
         def _():
             finish_q(0)
 
-    send_near(2)
+    last = HL - 1
+    last_kv[...] = all_cores(last).astype(BF16)
+    start(last_x)
+    r_lkv[y, 0] = last_kv[:SUB]
+    pack_dq(last, 0)
+    add_near(last)
+    for r in range(NY):
+        rows = slice(r * HS, (r + 1) * HS)
+        last_q[0, r] = dq32[last, 0, rows].astype(BF16)
+        for slot in range(1, 5):
+            last_q[slot, r] = dq16[last, slot, rows]
+    start(last_z)
+    r_lq[y, 0] = last_q[0, 0]
     finish_q(1)
-    finish_kv(2)
-    finish_q(2)
     start([fq_copy(r) for r in order])
     r_fq[y] = fin_q[0]
-    arrive([fkv_copy(h, r) for h in range(HL) for r in order] + [fq_copy(r) for r in order])
-    out_kv[...] = r_kv[...]
-    out_q[...] = r_fq[...]
+    arrive(last_x)
+    for n in range(NY):
+        total = r_lkv[n, 0].astype(F32)
+        for slot in range(1, NX):
+            total = total + r_lkv[n, slot].astype(F32)
+        out_kv[last, n] = total.astype(BF16)
+    arrive(last_z)
+    for n in range(NY):
+        total = r_lq[n, 0].astype(F32)
+        for slot in range(1, 5):
+            total = total + r_lq[n, slot].astype(F32)
+        out_q[n, :, last * D : HL * D] = unpack(total)
+    arrive([fkv_copy(h, r) for h in range(last) for r in order] + [fq_copy(r) for r in order])
+    for h in range(last):
+        out_kv[h] = r_kv[h]
+    out_q[:, :, : last * D] = r_fq[...]
 
     done = [y_copy(r, kind) for r in order for kind in range(3)]
     for step in range(1, NZ // 2 + 1):
@@ -403,10 +458,10 @@
                 done.append(s_copy(step, sign))
     done += [copy for r in range(NY) for copy in x_copies(r)]
     done += [c_copy(i) for i in range(NC)] + [kc_copy(h) for h in range(HL)]
-    done += [kx_copy(h, d) for h in range(HL) for d in X_SLOT if d]
-    done += [q_copy(h, d) for h in range(HL) for d in (2, -2, 1, -1)]
+    done += [kx_copy(h, d) for h in range(last) for d in X_SLOT if d]
+    done += [q_copy(h, d) for h in range(last) for d in (2, -2, 1, -1)] + last_x + last_z
     done += [v_copy(h, i) for h in range(HL) for i in range(4)]
-    done += [fkv_copy(h, r) for h in range(HL) for r in order] + [fq_copy(r) for r in order]
+    done += [fkv_copy(h, r) for h in range(last) for r in order] + [fq_copy(r) for r in order]
     for copy in done:
         copy.wait_send()
     for score in range(2):
@@ -460,9 +515,13 @@
             vm((HL, 4, PK, 2 * D), BF16),
             vm((HL, 5, PK, 2 * D), BF16),
             vm((HL, CH, 2 * D), BF16),
-            vm((NY, SUB, HL * D), BF16),
-            vm((HL, NY, SUB, 2 * D), BF16),
-            vm((NY, SUB, HL * D), BF16),
+            vm((NY, SUB, 2 * D), BF16),
+            vm((HL - 1, NY, SUB, 2 * D), BF16),
+            vm((NY, SUB, 2 * D), BF16),
+            vm((HALF, 2 * D), BF16),
+            vm((NY, NX, SUB, 2 * D), BF16),
+            vm((5, NY, HS, 2 * D), BF16),
+            vm((NY, 5, HS, 2 * D), BF16),
             dma((NY, 3)), dma((NY, 3)),
             dma((2,)), dma((2,)),
             dma((2, NZ // 2 + 1, NY)), dma((2, NZ // 2 + 1, NY)),
@@ -473,7 +532,9 @@
             dma((HL, NX)), dma((HL, NX)),
             dma((HL, 4)), dma((HL, 4)),
             dma((HL, 5)), dma((HL, 5)),
-            dma((HL + 1, NY)), dma((HL + 1, NY)),
+            dma((HL, NY)), dma((HL, NY)),
+            dma((NX, NY)), dma((NX, NY)),
+            dma((5, NY)), dma((5, NY)),
         ],
         compiler_params=pltpu.CompilerParams(
             collective_id=0, has_side_effects=True, vmem_limit_bytes=56 << 20

time: 59.3 us -> 58.4 us (0.985); the launches traced: 58.3 us -> 58.2 us
  no operation moved by 1% of the time
where the time goes in v5:
time: 58.4 us; the launch traced here: 58.2 us
  Pallas kernels  57.6 us (99%)
  between operations  0.64 us (1%)
    pallas_call x1, Pallas kernels, local(): pl.pallas_call(kernel, out_shape=(pltpu.VMEM((HL, NY, SUB, 2 * D), BF16),...  56.8 us

profile of v5, /device:TPU:1, one launch (start us, length us, event | category | flops | bytes accessed | tf_op | source)
XLA Modules:
  0.0 58.2 jit_solution(13232105706088517346)
XLA Ops:
  0.6 56.8 %attention_grad.1 = (bf16[3,4,48,128]{3,2,1,0:T(8,128)(2,1)S(1)}, bf16[4,48,192]{2,1,0:T(8,128)(2,1)S(1)}) custom-call(bf16[48,768]{1,0:T(8,128)(2,1)} %q_ref.1, bf16[48,768]{1,0:T(8,128)(2,1)} %k_ref.1, bf16[48,768]{1,0:T(8,128)(2,1)} %v_ref.1, bf16[48,768]{1,0:T(8,128)(2,1)} %o_ref.1, bf16[48,768]{1,0:T(8,128)(2,1)} %g_ref.1, f32[3,192]{1,0:T(4,128)} %bitcast.1), custom_call_target="tpu_custom_call" | custom-call | tf_op jit(solution)/shard_map/attention_grad/pallas_call | solution.py:488
  57.4 0.8 %place.1 = (bf16[48,768]{1,0:T(8,128)(2,1)}, bf16[48,768]{1,0:T(8,128)(2,1)}, bf16[48,768]{1,0:T(8,128)(2,1)}) custom-call(bf16[3,4,48,128]{3,2,1,0:T(8,128)(2,1)S(1)} %get-tuple-element.5.kv_ref, bf16[4,48,192]{2,1,0:T(8,128)(2,1)S(1)} %get-tuple-element.6.q_ref), custom_call_target="tpu_custom_call" | custom-call | tf_op jit(solution)/shard_map/place/pallas_call | solution.py:545

commit v6 on v5

--- a/solution.py
+++ b/solution.py
@@ -40,7 +40,7 @@
 
 def kernel(
     q_ref, k_ref, v_ref, o_ref, g_ref, lse_ref, out_kv, out_q,
-    st_qg, st_kv, st_d, st_lse, qg, kv, r_lse, r_d, stat, stat_all, dqt, dkv, dkv16, r_core, x16,
+    st_qg, st_kv, st_d, st_lse, qg, kv, pair, r_lse, r_d, stat, stat_all, dqt, dkv, dkv16, r_core, x16,
     r_x, dq32, dq16, r_v, r_q, fin_kv, fin_q, r_kv, r_fq, last_kv, r_lkv, last_q, r_lq,
     a_send, a_recv, l_send, l_recv, z_send, z_recv, s_send, s_recv, x_send, x_recv, c_send, c_recv,
     kc_send, kc_recv, kx_send, kx_recv, v_send, v_recv, q_send, q_recv, f_send, f_recv,
@@ -75,8 +75,8 @@
             copy.wait_recv()
 
     barrier = pltpu.get_barrier_semaphore()
-    peers = [dev(dy=dy, other=o) for dy in range(NY) for o in (False, True) if dy or o]
-    peers += [dev(dz=d) for d in (1, -1, 2, -2)] + [dev(dx=d) for d in X_SLOT if d]
+    peers = [dev(dy=dy) for dy in range(1, NY)] + [dev(other=True), dev(dz=1), dev(dz=-1)]
+    peers += [dev(dx=d) for d in X_SLOT if d]
     for peer in peers:
         pl.semaphore_signal(barrier, inc=1, device_id=peer, device_id_type=MESH)
 
@@ -128,17 +128,14 @@
             c_send.at[i], c_recv.at[i], dev(other=True),
         )
 
-    lse_to = (g % 2) * (NX * NZ) + x * NZ + z
-    lse_own = core == y_lo
-
-    def lse_copy(score):
-        return remote(
-            st_lse.at[score], r_lse.at[y_lo], l_send.at[score], l_recv.at[y_lo],
-            (lse_to, (g // 2) * 2 + score),
-        )
-
-    def lse_local(score):
-        return lse_own & (core == score)
+    def lse_core():
+        return remote(
+            st_lse.at[1 - core], pair.at[core], l_send.at[0], l_recv.at[0], dev(other=True)
+        )
+
+    def lse_y():
+        there = (1 - y_lo) * (NX * NZ) + x * NZ + z
+        return remote(pair.at[1 - y_lo], r_lse.at[y_lo], l_send.at[1], l_recv.at[1], (there, g))
 
     def stage(st, left, right):
         for n in range(NY * HL):
@@ -149,6 +146,11 @@
     stage(st_kv, k_ref[...], v_ref[...])
     pl.semaphore_wait(barrier, len(peers))
     start([y_copy(r, 1) for r in order])
+    st_lse[...] = jnp.zeros_like(st_lse)
+    for s in range(NY):
+        st_lse[s % 2, s // 2, 0:HL] = lse_ref[:, s * SUB : (s + 1) * SUB]
+    lse_core().start()
+    pair[core] = st_lse[core]
     kv[:, 0:SUB] = st_kv[y]
     start(x_copies(0) + [c_copy(0)])
     gs = g_ref[...]
@@ -167,22 +169,12 @@
     for n in range(NY):
         st_d[n] = deltas[8 * n : 8 * n + 8]
     start([y_copy(r, 2) for r in order])
-    st_lse[...] = jnp.zeros_like(st_lse)
-    for s in range(NY):
-        st_lse[s % 2, s // 2, 0:HL] = lse_ref[:, s * SUB : (s + 1) * SUB]
-    for score in range(2):
-
-        @pl.when(jnp.logical_not(lse_local(score)))
-        def _():
-            lse_copy(score).start()
-
-        @pl.when(lse_local(score))
-        def _():
-            r_lse[y_lo] = st_lse[score]
-
     r_d[0] = st_d[y]
     dqt[...] = jnp.zeros_like(dqt)
     dkv[...] = jnp.zeros_like(dkv)
+    lse_core().wait_recv()
+    lse_y().start()
+    r_lse[y_lo] = pair[y_lo]
 
     for r, kind in ((1, 1), (3, 1), (1, 0), (3, 0), (2, 1), (2, 0)):
         y_copy(NY - r, kind).wait_recv()
@@ -192,19 +184,11 @@
             start([z_copy(1, 1, r), z_copy(1, -1, r)])
     for r in range(1, NY):
         y_copy(r, 2).wait_recv()
-    for source in range(2):
-
-        @pl.when(jnp.logical_not(lse_own & (source == y_lo)))
-        def _():
-            remote(
-                st_lse.at[0], r_lse.at[source], l_send.at[0], l_recv.at[source],
-                (lse_to, (g // 2) * 2),
-            ).wait_recv()
-
+    lse_y().wait_recv()
     for r in range(NY):
         from_at = (y + r) % NY
-        stat[0, 0:8, r * SUB : (r + 1) * SUB] = r_lse[from_at % 2, from_at // 2]
-        stat[0, 8:16, r * SUB : (r + 1) * SUB] = r_d[r]
+        both = jnp.concatenate([r_lse[from_at % 2, from_at // 2][:HL], r_d[r][: 8 - HL]], axis=0)
+        stat[0, :, r * SUB : (r + 1) * SUB] = both
     start([s_copy(1, 1), s_copy(1, -1)])
     for i, r in enumerate((0, 1, 3, 2)):
         arrive(x_copies(r))
@@ -379,7 +363,7 @@
         cols = pl.ds(pl.multiple_of(late * (4 * CH), 4 * CH), 4 * CH)
         js = pl.ds(pl.multiple_of(sib * HALF, HALF), HALF)
         norms = stat_all[pl.ds(h, 1), cols]
-        dels = stat_all[pl.ds(8 + h, 1), cols]
+        dels = stat_all[pl.ds(HL + h, 1), cols]
         rows_q = qg[h, cols]
         both = kv[h, js]
         zero = jnp.zeros_like(both)
@@ -450,7 +434,7 @@
         out_kv[h] = r_kv[h]
     out_q[:, :, : last * D] = r_fq[...]
 
-    done = [y_copy(r, kind) for r in order for kind in range(3)]
+    done = [y_copy(r, kind) for r in order for kind in range(3)] + [lse_core(), lse_y()]
     for step in range(1, NZ // 2 + 1):
         for sign in (1, -1):
             done += [z_copy(step, sign, r) for r in parts(step, sign)]
@@ -464,11 +448,6 @@
     done += [fkv_copy(h, r) for h in range(last) for r in order] + [fq_copy(r) for r in order]
     for copy in done:
         copy.wait_send()
-    for score in range(2):
-
-        @pl.when(jnp.logical_not(lse_local(score)))
-        def _():
-            lse_copy(score).wait_send()
 
 
 def place(kv_ref, q_ref, dq_ref, dk_ref, dv_ref):
@@ -501,9 +480,10 @@
             vm((HL, NI, 2 * D), BF16),
             vm((HL, NJ, 2 * D), BF16),
             vm((2, 2, 8, SUB), F32),
+            vm((2, 2, 8, SUB), F32),
             vm((NY, 8, SUB), F32),
-            vm((NZ, 16, CH), F32),
-            vm((16, NI), F32),
+            vm((NZ, 8, CH), F32),
+            vm((8, NI), F32),
             vm((HL, D, NI), F32),
             vm((HL, NJ, 2 * D), F32),
             vm((HL, HALF, 2 * D), BF16),

time: 58.4 us -> 57.8 us (0.990)
  Pallas kernels: 57.6 us -> 57 us
    pallas_call x1, Pallas kernels: 56.8 us -> 56.2 us  [local(): pl.pallas_call(kernel, out_shape=(pltpu.VMEM((HL, NY, SUB, 2 * D), BF16),...]
where the time goes in v6:
time: 57.8 us; the launch traced here: 57.6 us
  Pallas kernels  57 us (99%)
  between operations  0.64 us (1%)
    pallas_call x1, Pallas kernels, local(): pl.pallas_call(kernel, out_shape=(pltpu.VMEM((HL, NY, SUB, 2 * D), BF16),...  56.2 us

profile of v6, /device:TPU:1, one launch (start us, length us, event | category | flops | bytes accessed | tf_op | source)
XLA Modules:
  0.0 57.6 jit_solution(3368550594073892942)
XLA Ops:
  0.6 56.2 %attention_grad.1 = (bf16[3,4,48,128]{3,2,1,0:T(8,128)(2,1)S(1)}, bf16[4,48,192]{2,1,0:T(8,128)(2,1)S(1)}) custom-call(bf16[48,768]{1,0:T(8,128)(2,1)} %q_ref.1, bf16[48,768]{1,0:T(8,128)(2,1)} %k_ref.1, bf16[48,768]{1,0:T(8,128)(2,1)} %v_ref.1, bf16[48,768]{1,0:T(8,128)(2,1)} %o_ref.1, bf16[48,768]{1,0:T(8,128)(2,1)} %g_ref.1, f32[3,192]{1,0:T(4,128)} %bitcast.1), custom_call_target="tpu_custom_call" | custom-call | tf_op jit(solution)/shard_map/attention_grad/pallas_call | solution.py:467
  56.8 0.8 %place.1 = (bf16[48,768]{1,0:T(8,128)(2,1)}, bf16[48,768]{1,0:T(8,128)(2,1)}, bf16[48,768]{1,0:T(8,128)(2,1)}) custom-call(bf16[3,4,48,128]{3,2,1,0:T(8,128)(2,1)S(1)} %get-tuple-element.5.kv_ref, bf16[4,48,192]{2,1,0:T(8,128)(2,1)S(1)} %get-tuple-element.6.q_ref), custom_call_target="tpu_custom_call" | custom-call | tf_op jit(solution)/shard_map/place/pallas_call | solution.py:525

commit v7 on v6

--- a/solution.py
+++ b/solution.py
@@ -73,6 +73,10 @@
     def arrive(copies):
         for copy in copies:
             copy.wait_recv()
+
+    def leave(copies):
+        for copy in copies:
+            copy.wait_send()
 
     barrier = pltpu.get_barrier_semaphore()
     peers = [dev(dy=dy) for dy in range(1, NY)] + [dev(other=True), dev(dz=1), dev(dz=-1)]
@@ -392,20 +396,23 @@
         def _():
             send_x(h)
 
-        @pl.when((t == 8) | (t == 10))
-        def _():
-            send_near((t - 8) // 2)
-            finish_kv((t - 8) // 2)
+        @pl.when((t == 8) | (t == 9))
+        def _():
+            send_near(t - 8)
+            finish_kv(t - 8)
 
         @pl.when(t == 10)
         def _():
             finish_q(0)
 
     last = HL - 1
+    pack_dq(last, 0)
     last_kv[...] = all_cores(last).astype(BF16)
     start(last_x)
     r_lkv[y, 0] = last_kv[:SUB]
-    pack_dq(last, 0)
+    finish_q(1)
+    start([fq_copy(r) for r in order])
+    r_fq[y] = fin_q[0]
     add_near(last)
     for r in range(NY):
         rows = slice(r * HS, (r + 1) * HS)
@@ -414,26 +421,6 @@
             last_q[slot, r] = dq16[last, slot, rows]
     start(last_z)
     r_lq[y, 0] = last_q[0, 0]
-    finish_q(1)
-    start([fq_copy(r) for r in order])
-    r_fq[y] = fin_q[0]
-    arrive(last_x)
-    for n in range(NY):
-        total = r_lkv[n, 0].astype(F32)
-        for slot in range(1, NX):
-            total = total + r_lkv[n, slot].astype(F32)
-        out_kv[last, n] = total.astype(BF16)
-    arrive(last_z)
-    for n in range(NY):
-        total = r_lq[n, 0].astype(F32)
-        for slot in range(1, 5):
-            total = total + r_lq[n, slot].astype(F32)
-        out_q[n, :, last * D : HL * D] = unpack(total)
-    arrive([fkv_copy(h, r) for h in range(last) for r in order] + [fq_copy(r) for r in order])
-    for h in range(last):
-        out_kv[h] = r_kv[h]
-    out_q[:, :, : last * D] = r_fq[...]
-
     done = [y_copy(r, kind) for r in order for kind in range(3)] + [lse_core(), lse_y()]
     for step in range(1, NZ // 2 + 1):
         for sign in (1, -1):
@@ -443,11 +430,29 @@
     done += [copy for r in range(NY) for copy in x_copies(r)]
     done += [c_copy(i) for i in range(NC)] + [kc_copy(h) for h in range(HL)]
     done += [kx_copy(h, d) for h in range(last) for d in X_SLOT if d]
-    done += [q_copy(h, d) for h in range(last) for d in (2, -2, 1, -1)] + last_x + last_z
+    done += [q_copy(h, d) for h in range(last) for d in (2, -2, 1, -1)]
     done += [v_copy(h, i) for h in range(HL) for i in range(4)]
-    done += [fkv_copy(h, r) for h in range(last) for r in order] + [fq_copy(r) for r in order]
-    for copy in done:
-        copy.wait_send()
+    leave(done)
+    leave(last_x)
+    arrive(last_x)
+    for n in range(NY):
+        total = r_lkv[n, 0].astype(F32)
+        for slot in range(1, NX):
+            total = total + r_lkv[n, slot].astype(F32)
+        out_kv[last, n] = total.astype(BF16)
+    leave(last_z)
+    arrive(last_z)
+    for n in range(NY):
+        total = r_lq[n, 0].astype(F32)
+        for slot in range(1, 5):
+            total = total + r_lq[n, slot].astype(F32)
+        out_q[n, :, last * D : HL * D] = unpack(total)
+    fc = [fkv_copy(h, r) for h in range(last) for r in order] + [fq_copy(r) for r in order]
+    arrive(fc)
+    for h in range(last):
+        out_kv[h] = r_kv[h]
+    out_q[:, :, : last * D] = r_fq[...]
+    leave(fc)
 
 
 def place(kv_ref, q_ref, dq_ref, dk_ref, dv_ref):

time: 57.8 us -> 58 us (level)
  no operation moved by 1% of the time
where the time goes in v7:
time: 58 us; the launch traced here: 57.8 us
  Pallas kernels  57.2 us (99%)
  between operations  0.64 us (1%)
    pallas_call x1, Pallas kernels, local(): pl.pallas_call(kernel, out_shape=(pltpu.VMEM((HL, NY, SUB, 2 * D), BF16),...  56.4 us

profile of v7, /device:TPU:1, one launch (start us, length us, event | category | flops | bytes accessed | tf_op | source)
XLA Modules:
  0.0 57.8 jit_solution(11964714034748273088)
XLA Ops:
  0.6 56.4 %attention_grad.1 = (bf16[3,4,48,128]{3,2,1,0:T(8,128)(2,1)S(1)}, bf16[4,48,192]{2,1,0:T(8,128)(2,1)S(1)}) custom-call(bf16[48,768]{1,0:T(8,128)(2,1)} %q_ref.1, bf16[48,768]{1,0:T(8,128)(2,1)} %k_ref.1, bf16[48,768]{1,0:T(8,128)(2,1)} %v_ref.1, bf16[48,768]{1,0:T(8,128)(2,1)} %o_ref.1, bf16[48,768]{1,0:T(8,128)(2,1)} %g_ref.1, f32[3,192]{1,0:T(4,128)} %bitcast.1), custom_call_target="tpu_custom_call" | custom-call | tf_op jit(solution)/shard_map/attention_grad/pallas_call | solution.py:472
  57.0 0.8 %place.1 = (bf16[48,768]{1,0:T(8,128)(2,1)}, bf16[48,768]{1,0:T(8,128)(2,1)}, bf16[48,768]{1,0:T(8,128)(2,1)}) custom-call(bf16[3,4,48,128]{3,2,1,0:T(8,128)(2,1)S(1)} %get-tuple-element.5.kv_ref, bf16[4,48,192]{2,1,0:T(8,128)(2,1)S(1)} %get-tuple-element.6.q_ref), custom_call_target="tpu_custom_call" | custom-call | tf_op jit(solution)/shard_map/place/pallas_call | solution.py:530

commit v8 on v7

--- a/solution.py
+++ b/solution.py
@@ -262,6 +262,7 @@
         add_near(h)
         start([q_copy(h, d) for d in (2, -2, 1, -1)])
 
+    last = HL - 1
     NEAR = (2, -2, 1, -1, 0)
     FAR_X = (2, 1, -1, 0)
 
@@ -314,8 +315,11 @@
             dev(dy=r),
         )
 
-    def fq_copy(r):
-        return remote(fin_q.at[r], r_fq.at[y], f_send.at[HL - 1, r], f_recv.at[HL - 1, r], dev(dy=r))
+    def fq_copy(h, r):
+        return remote(
+            fin_q.at[h, r], r_fq.at[h, y], f_send.at[last + h, r], f_recv.at[last + h, r],
+            dev(dy=r),
+        )
 
     def finish_kv(h):
         arrive([kx_copy(h, d) for d in X_SLOT if d])
@@ -336,7 +340,9 @@
         for slot in range(1, 5):
             total = total + r_q[h, slot].astype(F32)
         for r in range(NY):
-            fin_q[r, :, h * D : (h + 1) * D] = unpack(total[r * HS : (r + 1) * HS])
+            fin_q[h, r] = unpack(total[r * HS : (r + 1) * HS])
+        start([fq_copy(h, r) for r in order])
+        r_fq[h, y] = fin_q[h, 0]
 
     lane = lax.broadcasted_iota(jnp.int32, (HALF, 2 * D), 1)
 
@@ -405,14 +411,10 @@
         def _():
             finish_q(0)
 
-    last = HL - 1
     pack_dq(last, 0)
     last_kv[...] = all_cores(last).astype(BF16)
     start(last_x)
     r_lkv[y, 0] = last_kv[:SUB]
-    finish_q(1)
-    start([fq_copy(r) for r in order])
-    r_fq[y] = fin_q[0]
     add_near(last)
     for r in range(NY):
         rows = slice(r * HS, (r + 1) * HS)
@@ -433,6 +435,7 @@
     done += [q_copy(h, d) for h in range(last) for d in (2, -2, 1, -1)]
     done += [v_copy(h, i) for h in range(HL) for i in range(4)]
     leave(done)
+    finish_q(1)
     leave(last_x)
     arrive(last_x)
     for n in range(NY):
@@ -447,11 +450,12 @@
         for slot in range(1, 5):
             total = total + r_lq[n, slot].astype(F32)
         out_q[n, :, last * D : HL * D] = unpack(total)
-    fc = [fkv_copy(h, r) for h in range(last) for r in order] + [fq_copy(r) for r in order]
+    fc = [fkv_copy(h, r) for h in range(last) for r in order] + [fq_copy(h, r) for h in range(last) for r in order]
     arrive(fc)
     for h in range(last):
         out_kv[h] = r_kv[h]
-    out_q[:, :, : last * D] = r_fq[...]
+    for h in range(last):
+        out_q[:, :, h * D : (h + 1) * D] = r_fq[h]
     leave(fc)
 
 
@@ -500,9 +504,9 @@
             vm((HL, 4, PK, 2 * D), BF16),
             vm((HL, 5, PK, 2 * D), BF16),
             vm((HL, CH, 2 * D), BF16),
-            vm((NY, SUB, 2 * D), BF16),
+            vm((HL - 1, NY, SUB, D), BF16),
             vm((HL - 1, NY, SUB, 2 * D), BF16),
-            vm((NY, SUB, 2 * D), BF16),
+            vm((HL - 1, NY, SUB, D), BF16),
             vm((HALF, 2 * D), BF16),
             vm((NY, NX, SUB, 2 * D), BF16),
             vm((5, NY, HS, 2 * D), BF16),
@@ -517,7 +521,7 @@
             dma((HL, NX)), dma((HL, NX)),
             dma((HL, 4)), dma((HL, 4)),
             dma((HL, 5)), dma((HL, 5)),
-            dma((HL, NY)), dma((HL, NY)),
+            dma((2 * HL - 2, NY)), dma((2 * HL - 2, NY)),
             dma((NX, NY)), dma((NX, NY)),
             dma((5, NY)), dma((5, NY)),
         ],

time: 58 us -> 57 us (0.983)
  Pallas kernels: 57.2 us -> 56.2 us
    pallas_call x1, Pallas kernels: 56.4 us -> 55.4 us  [local(): pl.pallas_call(kernel, out_shape=(pltpu.VMEM((HL, NY, SUB, 2 * D), BF16),...]
where the time goes in v8:
time: 57 us; the launch traced here: 56.8 us
  Pallas kernels  56.2 us (99%)
  between operations  0.64 us (1%)
    pallas_call x1, Pallas kernels, local(): pl.pallas_call(kernel, out_shape=(pltpu.VMEM((HL, NY, SUB, 2 * D), BF16),...  55.4 us

profile of v8, /device:TPU:1, one launch (start us, length us, event | category | flops | bytes accessed | tf_op | source)
XLA Modules:
  0.0 56.8 jit_solution(16192076805920743112)
XLA Ops:
  0.6 55.4 %attention_grad.1 = (bf16[3,4,48,128]{3,2,1,0:T(8,128)(2,1)S(1)}, bf16[4,48,192]{2,1,0:T(8,128)(2,1)S(1)}) custom-call(bf16[48,768]{1,0:T(8,128)(2,1)} %q_ref.1, bf16[48,768]{1,0:T(8,128)(2,1)} %k_ref.1, bf16[48,768]{1,0:T(8,128)(2,1)} %v_ref.1, bf16[48,768]{1,0:T(8,128)(2,1)} %o_ref.1, bf16[48,768]{1,0:T(8,128)(2,1)} %g_ref.1, f32[3,192]{1,0:T(4,128)} %bitcast.1), custom_call_target="tpu_custom_call" | custom-call | tf_op jit(solution)/shard_map/attention_grad/pallas_call | solution.py:476
  56.0 0.8 %place.1 = (bf16[48,768]{1,0:T(8,128)(2,1)}, bf16[48,768]{1,0:T(8,128)(2,1)}, bf16[48,768]{1,0:T(8,128)(2,1)}) custom-call(bf16[3,4,48,128]{3,2,1,0:T(8,128)(2,1)S(1)} %get-tuple-element.5.kv_ref, bf16[4,48,192]{2,1,0:T(8,128)(2,1)S(1)} %get-tuple-element.6.q_ref), custom_call_target="tpu_custom_call" | custom-call | tf_op jit(solution)/shard_map/place/pallas_call | solution.py:534
